TPU v7x, 128 devices: a whole 4x4x4 slice. The times are simulated.
128 devices in a mesh: graph: 32 (over x, y, core), mp: 4 (over z).
Axes of the slice: x: 4, y: 4, z: 4, core: 2. Of those that a mesh axis runs over, the one named last changes fastest.
Arguments:
- edge_feats: bfloat16 [262144, 512], P('graph', 'mp'), may hold values from -6 to 6
- edge_source: int32 [262144], P('graph'), may hold values from 0 to 65535, as said below
- edge_target: int32 [262144], P('graph'), may hold values from 0 to 65535, as said below
- edge_live: int32 [262144], P('graph'), may hold values from 0 to 1, as said below
- trip_partner: int32 [8, 262144], P(None, 'graph'), may hold values from 0 to 262143, as said below
- trip_mask: int32 [8, 262144], P(None, 'graph'), may hold values 0 or 1
- trip_basis: bfloat16 [262144, 128], P('graph'), may hold values from -6 to 6
- atom_feats: bfloat16 [65536, 512], P('graph', 'mp'), may hold values from -6 to 6
- w_msg: bfloat16 [512, 512], P(None, 'mp'), may hold values from -0.25 to 0.25
- w_down: bfloat16 [512, 64], replicated, may hold values from -0.25 to 0.25
- w_bil: bfloat16 [1024, 64], replicated, may hold values from -0.1875 to 0.1875
- w_up: bfloat16 [64, 512], P(None, 'mp'), may hold values from -0.75 to 0.75
- w_atom: bfloat16 [512, 512], P(None, 'mp'), may hold values from -0.25 to 0.25
- w_edge: bfloat16 [512, 512], P(None, 'mp'), may hold values from -0.25 to 0.25
Outputs:
- edge_out: bfloat16 [262144, 512], P('graph', 'mp')
- atom_out: bfloat16 [65536, 512], P('graph', 'mp')
Inputs may be any that keep to these rules, and one draw needn't show every extreme that they name: `edge_target`: edge slots lie in blocks of 256: the slots of graph shard g for destination shard d are slots (g * 32 + d) * 256 onward; every source atom of shard g's slots lies in atoms g * 2048 to (g + 1) * 2048 - 1, every target atom of a block for d in shard d's atoms. `edge_source`: source atoms belong to the shard that holds the slot. `edge_live`: in each block of 256 slots the live slots come first, at least one; in every draw some destination shard gets all 256 slots live from every source shard. `trip_partner`: A partner edge is a slot of the same block of 256 slots as the edge.
All inputs are finite; a program needn't handle non-finite values. No bound on the sum of `trip_mask` on one device may be relied on, other than what follows from the above.
Results may differ from a plain program's by a relative error of at most 0.01.
Values may be sent and summed in bfloat16 or wider, within the bound.
A program may use at most 192 MiB of HBM per device.

v0:
```python
import math

import jax
import jax.numpy as jnp
from jax import lax
from jax.sharding import PartitionSpec as P

DT = 64
NB = 16
SLOTS = 8
CAP = 256


def local(
    edge_feats,
    edge_source,
    edge_target,
    edge_live,
    trip_partner,
    trip_mask,
    trip_basis,
    atom_feats,
    w_msg,
    w_down,
    w_bil,
    w_up,
    w_atom,
    w_edge,
):
    rows = edge_feats.shape[0]
    width = edge_feats.shape[1]
    atoms_local = atom_feats.shape[0]
    shard = lax.axis_index("graph")
    piece = lax.all_gather(edge_feats, "mp", axis=1, tiled=True)
    hid = jnp.dot(piece, w_msg, preferred_element_type=jnp.float32)
    down = jnp.dot(piece, w_down, preferred_element_type=jnp.float32)
    message = edge_feats.astype(jnp.float32) + jax.nn.silu(hid)
    down_rows = down.astype(jnp.bfloat16)
    blocks = rows // CAP
    group = math.gcd(blocks, 8)
    within_ids = jnp.transpose(trip_partner % CAP).reshape(blocks // group, group, CAP * SLOTS)
    down_blocks = down_rows.reshape(blocks // group, group, CAP, DT)
    columns = jnp.arange(CAP, dtype=jnp.int32)

    def pick_group(operands):
        ids, table = operands
        onehot = (ids[:, :, None] == columns[None, None, :]).astype(jnp.bfloat16)
        return jnp.einsum("gqc,gca->gqa", onehot, table, preferred_element_type=jnp.float32).astype(
            jnp.bfloat16
        )

    picked = lax.map(pick_group, (within_ids, down_blocks)).reshape(rows, SLOTS, DT)
    weights = (
        trip_basis.reshape(rows, SLOTS, NB)
        * jnp.transpose(trip_mask).astype(jnp.bfloat16)[:, :, None]
    )
    mixed = jnp.einsum("esb,esa->eba", weights, picked, preferred_element_type=jnp.float32).astype(
        jnp.bfloat16
    )
    bil = jnp.dot(mixed.reshape(rows, NB * DT), w_bil, preferred_element_type=jnp.float32).astype(
        jnp.bfloat16
    )
    total = message + jnp.dot(bil, w_up, preferred_element_type=jnp.float32)
    outgoing = (total * edge_live.astype(jnp.float32)[:, None]).astype(jnp.bfloat16)
    target_local = edge_target % atoms_local
    incoming, in_ids = (
        lax.all_to_all(outgoing, "graph", split_axis=0, concat_axis=0, tiled=True),
        lax.all_to_all(target_local, "graph", split_axis=0, concat_axis=0, tiled=True),
    )
    block = math.gcd(atoms_local, 512)

    def agg_block(index):
        ids = index * block + jnp.arange(block, dtype=jnp.int32)
        onehot = (ids[:, None] == in_ids[None, :]).astype(jnp.bfloat16)
        return jnp.dot(onehot, incoming, preferred_element_type=jnp.float32)

    agg = lax.map(agg_block, jnp.arange(atoms_local // block, dtype=jnp.int32)).reshape(
        atoms_local, width
    )
    atom_mid = (atom_feats.astype(jnp.float32) + agg).astype(jnp.bfloat16)
    ahid = jnp.dot(
        lax.all_gather(atom_mid, "mp", axis=1, tiled=True),
        w_atom,
        preferred_element_type=jnp.float32,
    )
    atom_out = (atom_mid.astype(jnp.float32) + jax.nn.silu(ahid)).astype(jnp.bfloat16)
    source_rows = jnp.take(atom_out, edge_source - shard * atoms_local, axis=0)
    everything = lax.all_gather(atom_out, "graph", axis=0, tiled=True)
    target_rows = jnp.take(everything, edge_target, axis=0)
    pair = (source_rows.astype(jnp.float32) * target_rows.astype(jnp.float32)).astype(jnp.bfloat16)
    ehid = jnp.dot(
        lax.all_gather(pair, "mp", axis=1, tiled=True), w_edge, preferred_element_type=jnp.float32
    )
    edge_out = (total + jax.nn.silu(ehid)).astype(jnp.bfloat16)
    return (edge_out, atom_out)


def solution(mesh):
    return jax.shard_map(
        local,
        mesh=mesh,
        in_specs=(
            P("graph", "mp"),
            P("graph"),
            P("graph"),
            P("graph"),
            P(None, "graph"),
            P(None, "graph"),
            P("graph", None),
            P("graph", "mp"),
            P(None, "mp"),
            P(),
            P(),
            P(None, "mp"),
            P(None, "mp"),
            P(None, "mp"),
        ),
        out_specs=(P("graph", "mp"), P("graph", "mp")),
        check_vma=False,
    )
```

profile of v0, /device:TPU:0, one launch (start us, length us, event | category | flops | bytes accessed | tf_op | source)
XLA Modules:
  0.0 530.0 jit_solution(10685544589907286826)
XLA Ops:
  7.2 0.0 copy-start
  7.2 0.0 copy-start.4
  7.2 0.0 all-gather.5.cloned.1.call-start
  7.2 0.7 all-gather.5.cloned.1.call-update
  7.9 1.4 fusion.21
  9.3 7.4 %all-to-all-start = ((s32[32,256,1]{1,2,0:T(1,128)}), s32[32,256,1]{1,2,0:T(1,128)S(1)}, u32[]{:S(2)}, u32[]{:S(2)}) async-start(s32[32,256,1]{1,2,0:T(1,128)} %bitcast.7), calls=%async_computation | async-start | bytes 65536 | tf_op jit(solution)/shard_map/all_to_all | solution.py:68
  16.8 0.8 convert_element_type.60
  17.5 4.1 copy.25
  21.6 0.0 copy-done.4
  21.6 0.1 fusion.19
  21.7 0.0 copy-start.3
  21.7 2.7 copy.26
  24.4 4.0 reshape.49
  28.5 0.0 copy-done.3
  28.5 1.9 broadcast_multiply_fusion
  30.4 0.0 copy-start.8
  30.4 13.1 %copy.29 = bf16[8192,8,16]{2,1,0:T(8,128)(2,1)} copy(bf16[8192,8,16]{0,2,1:T(8,128)(2,1)S(1)} %broadcast_multiply_fusion) | data formatting | bytes 4194304 | tf_op jit(solution)/shard_map/mul | solution.py:54
  43.5 55.8 %all-gather.5.cloned.1.call-done = bf16[8192,512]{1,0:T(8,128)(2,1)} async-done(((bf16[8192,128]{1,0:T(8,128)(2,1)}), bf16[8192,512]{1,0:T(8,128)(2,1)}) %all-gather.5.cloned.1.call-update) | async-done | bytes 8388624 | tf_op jit(solution)/shard_map/all_gather | solution.py:34
  99.3 0.0 copy-done.8
  99.3 6.0 %convolution_convert_fusion.2 = bf16[8192,64]{0,1:T(8,128)(2,1)S(1)} fusion(bf16[8192,512]{1,0:T(8,128)(2,1)} %all-gather.5.cloned.1.call-done, bf16[512,64]{0,1:T(8,128)(2,1)S(1)} %copy-done.8), kind=kOutput, calls=%fused_computation.22 | convolution fusion | flops 537395200 | bytes 9502720 | tf_op jit(solution)/shard_map/dot_general | solution.py:36
  105.3 0.3 copy.33
  105.5 22.7 %while.22 = (s32[]{:T(128)}, bf16[4,8,2048,64]{2,3,1,0:T(8,128)(2,1)}, s32[4,8,2048]{2,1,0:T(8,128)S(1)}, bf16[4,8,256,64]{2,1,0,3:T(8,128)(2,1)S(1)}, s32[]{:T(128)}) while((s32[]{:T(128)}, bf16[4,8,2048,64]{2,3,1,0:T(8,128)(2,1)}, s32[4,8,2048]{2,1,0:T(8,128)S(1)}, bf16[4,8,256,64]{2,1,0,3:T(8,128)(2,1)S(1)}, s32[]{:T(128)}) %tuple.57), condition=%wide.region_1.2_spmd.clone, body=%wide.region_0.1_spmd.clone.sunk | while | flops 542113792 | bytes 3080273 | solution.py:52
  105.6 5.6 %fusion.45 = bf16[4,8,2048,64]{2,3,1,0:T(8,128)(2,1)} fusion(bf16[4,8,2048,64]{2,3,1,0:T(8,128)(2,1)} %get-tuple-element.164, s32[]{:T(128)S(6)} %copy.42, s32[8,2048]{1,0:T(8,128)S(1)} %dynamic-slice_bitcast_fusion.2, bf16[1,8,256,64]{2,1,0,3:T(8,128)(2,1)S(1)} %constant_dynamic-slice_fusion.2), kind=kOutput, calls=%fused_computation.15.clone.1 | convolution fusion | flops 542113792 | bytes 2424836 | tf_op jit(solution)/shard_map/while/body/eval_jaxpr/gqc,gca->gqa/dot_general | solution.py:48
  111.3 5.6 %fusion.45 = bf16[4,8,2048,64]{2,3,1,0:T(8,128)(2,1)} fusion(bf16[4,8,2048,64]{2,3,1,0:T(8,128)(2,1)} %get-tuple-element.164, s32[]{:T(128)S(6)} %copy.42, s32[8,2048]{1,0:T(8,128)S(1)} %dynamic-slice_bitcast_fusion.2, bf16[1,8,256,64]{2,1,0,3:T(8,128)(2,1)S(1)} %constant_dynamic-slice_fusion.2), kind=kOutput, calls=%fused_computation.15.clone.1 | convolution fusion | flops 542113792 | bytes 2424836 | tf_op jit(solution)/shard_map/while/body/eval_jaxpr/gqc,gca->gqa/dot_general | solution.py:48
  117.0 5.6 %fusion.45 = bf16[4,8,2048,64]{2,3,1,0:T(8,128)(2,1)} fusion(bf16[4,8,2048,64]{2,3,1,0:T(8,128)(2,1)} %get-tuple-element.164, s32[]{:T(128)S(6)} %copy.42, s32[8,2048]{1,0:T(8,128)S(1)} %dynamic-slice_bitcast_fusion.2, bf16[1,8,256,64]{2,1,0,3:T(8,128)(2,1)S(1)} %constant_dynamic-slice_fusion.2), kind=kOutput, calls=%fused_computation.15.clone.1 | convolution fusion | flops 542113792 | bytes 2424836 | tf_op jit(solution)/shard_map/while/body/eval_jaxpr/gqc,gca->gqa/dot_general | solution.py:48
  122.6 5.6 %fusion.45 = bf16[4,8,2048,64]{2,3,1,0:T(8,128)(2,1)} fusion(bf16[4,8,2048,64]{2,3,1,0:T(8,128)(2,1)} %get-tuple-element.164, s32[]{:T(128)S(6)} %copy.42, s32[8,2048]{1,0:T(8,128)S(1)} %dynamic-slice_bitcast_fusion.2, bf16[1,8,256,64]{2,1,0,3:T(8,128)(2,1)S(1)} %constant_dynamic-slice_fusion.2), kind=kOutput, calls=%fused_computation.15.clone.1 | convolution fusion | flops 542113792 | bytes 2424836 | tf_op jit(solution)/shard_map/while/body/eval_jaxpr/gqc,gca->gqa/dot_general | solution.py:48
  128.3 15.6 %copy.28 = bf16[4,8,2048,64]{3,2,1,0:T(8,128)(2,1)} copy(bf16[4,8,2048,64]{2,3,1,0:T(8,128)(2,1)} %get-tuple-element.56) | data formatting | bytes 16777216 | tf_op jit(solution)/shard_map/while | solution.py:52
  143.8 26.9 %convolution_convert_fusion = bf16[8192,16,64]{2,1,0:T(8,128)(2,1)} fusion(bf16[8192,8,16]{2,1,0:T(8,128)(2,1)} %copy.29, bf16[8192,8,64]{2,1,0:T(8,128)(2,1)} %bitcast.60), kind=kOutput, calls=%fused_computation.19 | convolution fusion | flops 142606336 | bytes 27262976 | tf_op jit(solution)/shard_map/esb,esa->eba/dot_general | solution.py:57
  170.7 35.4 %copy.30 = bf16[8192,16,64]{0,2,1:T(8,128)(2,1)} copy(bf16[8192,16,64]{2,1,0:T(8,128)(2,1)} %convolution_convert_fusion) | data formatting | bytes 33554432 | tf_op jit(solution)/shard_map/convert_element_type | solution.py:57
  206.1 0.0 copy-done.5
  206.1 7.8 %fusion.23 = f32[8192,128]{1,0:T(8,128)} fusion(bf16[8192,512]{1,0:T(8,128)(2,1)} %all-gather.5.cloned.1.call-done, bf16[512,128]{1,0:T(8,128)(2,1)S(1)} %copy-done.5), kind=kOutput, calls=%fused_computation.46 | convolution fusion | flops 1073741824 | bytes 12713984 | tf_op jit(solution)/shard_map/dot_general | solution.py:35
  214.0 0.0 copy-done
  214.0 0.0 copy-done.2
  214.0 0.0 copy-done.11
  214.0 11.0 %multiply_convert_fusion.1 = (bf16[8192,128]{1,0:T(8,128)(2,1)}, f32[8192,128]{1,0:T(8,128)}) fusion(f32[8192]{0:T(1024)S(1)} %convert_element_type.60, bf16[64,128]{1,0:T(8,128)(2,1)S(1)} %copy-done.11, bf16[1024,64]{0,1:T(8,128)(2,1)S(1)} %copy-done, bf16[8192,1024]{0,1:T(8,128)(2,1)} %bitcast.61, f32[8192,128]{1,0:T(8,128)} %fusion.23, ...), kind=kOutput, calls=%fused_computation.25 | convolution fusion | flops 1217921024 | bytes 29540352 | tf_op jit(solution)/shard_map/dot_general | solution.py:63
  225.0 0.0 all-to-all-done
  225.0 7.1 %all-to-all-start.1 = ((bf16[32,256,128]{2,1,0:T(8,128)(2,1)}), bf16[32,256,128]{2,1,0:T(8,128)(2,1)S(1)}, u32[]{:S(2)}, u32[]{:S(2)}) async-start(bf16[32,256,128]{2,1,0:T(8,128)(2,1)} %bitcast.66), calls=%async_computation.1 | async-start | bytes 4194304 | tf_op jit(solution)/shard_map/all_to_all | solution.py:67
  232.1 0.2 all-gather.7.cloned.1.call-start
  232.3 28.7 %all-to-all-done.1 = bf16[32,256,128]{2,1,0:T(8,128)(2,1)S(1)} async-done(((bf16[32,256,128]{2,1,0:T(8,128)(2,1)}), bf16[32,256,128]{2,1,0:T(8,128)(2,1)S(1)}, u32[]{:S(2)}, u32[]{:S(2)}) %all-to-all-start.1) | async-done | bytes 2097184 | tf_op jit(solution)/shard_map/all_to_all | solution.py:67
  261.0 14.6 %while.21 = (s32[]{:T(128)}, f32[4,512,128]{2,1,0:T(8,128)S(1)}, s32[4]{0:T(128)S(1)}, s32[8192]{0:T(1024)S(1)}, bf16[8192,128]{1,0:T(8,128)(2,1)S(1)}, /*index=5*/s32[]{:T(128)}, s32[1]{0:T(128)}) while((s32[]{:T(128)}, f32[4,512,128]{2,1,0:T(8,128)S(1)}, s32[4]{0:T(128)S(1)}, s32[8192]{0:T(1024)S(1)}, bf16[8192,128]{1,0:T(8,128)(2,1)S(1)}, ...), condition=%wide.region_3.4_spmd, body=%wide.region_2.3_spmd.sunk | while | flops 1077936640 | bytes 2396277 | solution.py:77
  261.0 0.6 dynamic_slice.19
  262.2 2.4 fusion.44
  264.6 0.6 dynamic_slice.19
  265.9 2.4 fusion.44
  268.3 0.6 dynamic_slice.19
  269.5 2.4 fusion.44
  271.9 0.6 dynamic_slice.19
  273.2 2.4 fusion.44
  275.6 2.1 fusion.17
  277.6 0.0 all-gather.7.cloned.1.call-update
  277.7 0.0 all-gather.9.cloned.1.call-start
  277.7 30.6 %all-gather.7.cloned.1.call-done = bf16[2048,512]{1,0:T(8,128)(2,1)} async-done(((bf16[2048,128]{1,0:T(8,128)(2,1)}), bf16[2048,512]{1,0:T(8,128)(2,1)}) %all-gather.7.cloned.1.call-update) | async-done | bytes 2097168 | tf_op jit(solution)/shard_map/all_gather | solution.py:82
  308.3 3.2 add_convert_fusion.1
  311.5 0.0 all-gather.9.cloned.1.call-update
  311.5 0.0 all-gather.11.cloned.1.call-start
  311.6 0.9 copy-done.1
  312.5 24.0 %gather_fusion = bf16[8192,128]{1,0:T(8,128)(2,1)S(1)} fusion(bf16[2048,128]{1,0:T(8,128)(2,1)S(1)} %copy-done.1, s32[8192]{0:T(1024)S(1)} %fusion.22), kind=kCustom, calls=%fused_computation | custom fusion | bytes 4227072 | tf_op jit(solution)/shard_map/jit(_take)/gather | solution.py:87
  336.6 48.3 %all-gather.9.cloned.1.call-done = bf16[65536,128]{1,0:T(8,128)(2,1)} async-done(((bf16[2048,128]{1,0:T(8,128)(2,1)}), bf16[65536,128]{1,0:T(8,128)(2,1)}) %all-gather.9.cloned.1.call-update) | async-done | bytes 16777232 | tf_op jit(solution)/shard_map/all_gather | solution.py:88
  384.9 36.2 %gather_fusion.1 = bf16[8192,128]{1,0:T(8,128)(2,1)} fusion(bf16[65536,128]{1,0:T(8,128)(2,1)} %all-gather.9.cloned.1.call-done, s32[8192]{0:T(1024)S(1)} %get-tuple-element.98), kind=kCustom, calls=%fused_computation.1 | custom fusion | bytes 4227072 | tf_op jit(solution)/shard_map/jit(_take)/gather | solution.py:89
  421.0 7.4 %multiply_convert_fusion = bf16[8192,128]{1,0:T(8,128)(2,1)} fusion(bf16[8192,128]{1,0:T(8,128)(2,1)} %gather_fusion.1, bf16[8192,128]{1,0:T(8,128)(2,1)S(1)} %gather_fusion, pred[8192]{0:T(1024)(128)(4,1)S(1)} %compare_and_fusion, pred[8192]{0:T(1024)(128)(4,1)S(1)} %compare_and_fusion.1), kind=kLoop, calls=%fused_computation.24 | loop fusion | flops 6291456 | bytes 6307840 | tf_op jit(solution)/shard_map/convert_element_type | solution.py:90
  428.4 0.0 all-gather.11.cloned.1.call-update
  428.4 86.8 %all-gather.11.cloned.1.call-done = bf16[8192,512]{1,0:T(8,128)(2,1)} async-done(((bf16[8192,128]{1,0:T(8,128)(2,1)}), bf16[8192,512]{1,0:T(8,128)(2,1)}) %all-gather.11.cloned.1.call-update) | async-done | bytes 8388624 | tf_op jit(solution)/shard_map/all_gather | solution.py:92
  515.2 0.0 copy-done.10
  515.2 8.3 %add_convert_fusion = bf16[8192,128]{1,0:T(8,128)(2,1)} fusion(f32[8192,128]{1,0:T(8,128)} %get-tuple-element.101, bf16[8192,512]{1,0:T(8,128)(2,1)} %all-gather.11.cloned.1.call-done, bf16[512,128]{1,0:T(8,128)(2,1)S(1)} %copy-done.10), kind=kOutput, calls=%fused_computation.23 | convolution fusion | flops 1080033280 | bytes 14811136 | tf_op jit(solution)/shard_map/dot_general | solution.py:91
  (30 shorter events, 0.3 us)
Async XLA Ops:
  7.2 206.8 %copy-start = (bf16[1024,64]{0,1:T(8,128)(2,1)S(1)}, bf16[1024,64]{0,1:T(8,128)(2,1)}, u32[]{:S(2)}) copy-start(bf16[1024,64]{0,1:T(8,128)(2,1)} %param.28) | copy-start | bytes 393220
  7.2 14.4 %copy-start.4 = (s32[8,8192]{1,0:T(8,128)S(1)}, s32[8,8192]{1,0:T(8,128)}, u32[]{:S(2)}) copy-start(s32[8,8192]{1,0:T(8,128)} %param.22) | copy-start | bytes 786436
  7.2 92.1 %all-gather.5.cloned.1.call-start = ((), (), s32[]{:S(2)}) async-start(), calls=%async_computation.2 | async-start | bytes 10485760 | tf_op jit(solution)/shard_map/all_gather | solution.py:34
  9.3 215.6 %all-to-all-start = ((s32[32,256,1]{1,2,0:T(1,128)}), s32[32,256,1]{1,2,0:T(1,128)S(1)}, u32[]{:S(2)}, u32[]{:S(2)}) async-start(s32[32,256,1]{1,2,0:T(1,128)} %bitcast.7), calls=%async_computation | async-start | bytes 65536 | tf_op jit(solution)/shard_map/all_to_all | solution.py:68
  21.7 6.8 %copy-start.3 = (s32[8,8192]{1,0:T(8,128)S(1)}, s32[8,8192]{1,0:T(8,128)}, u32[]{:S(2)}) copy-start(s32[8,8192]{1,0:T(8,128)} %param.23) | copy-start | bytes 786436
  30.4 68.9 %copy-start.8 = (bf16[512,64]{0,1:T(8,128)(2,1)S(1)}, bf16[512,64]{0,1:T(8,128)(2,1)}, u32[]{:S(2)}) copy-start(bf16[512,64]{0,1:T(8,128)(2,1)} %param.27) | copy-start | bytes 196612
  170.7 35.4 %copy-start.5 = (bf16[512,128]{1,0:T(8,128)(2,1)S(1)}, bf16[512,128]{1,0:T(8,128)(2,1)}, u32[]{:S(2)}) copy-start(bf16[512,128]{1,0:T(8,128)(2,1)} %param.26) | copy-start | bytes 393220
  206.1 7.9 %copy-start.2 = (bf16[8192,128]{1,0:T(8,128)(2,1)S(1)}, bf16[8192,128]{1,0:T(8,128)(2,1)}, u32[]{:S(2)}) copy-start(bf16[8192,128]{1,0:T(8,128)(2,1)} %param.18) | copy-start | bytes 6291460
  206.1 7.9 %copy-start.11 = (bf16[64,128]{1,0:T(8,128)(2,1)S(1)}, bf16[64,128]{1,0:T(8,128)(2,1)}, u32[]{:S(2)}) copy-start(bf16[64,128]{1,0:T(8,128)(2,1)} %param.29) | copy-start | bytes 49156
  225.0 36.0 %all-to-all-start.1 = ((bf16[32,256,128]{2,1,0:T(8,128)(2,1)}), bf16[32,256,128]{2,1,0:T(8,128)(2,1)S(1)}, u32[]{:S(2)}, u32[]{:S(2)}) async-start(bf16[32,256,128]{2,1,0:T(8,128)(2,1)} %bitcast.66), calls=%async_computation.1 | async-start | bytes 4194304 | tf_op jit(solution)/shard_map/all_to_all | solution.py:67
  232.1 76.2 %all-gather.7.cloned.1.call-start = ((), (), s32[]{:S(2)}) async-start(), calls=%async_computation.3 | async-start | bytes 2621440 | tf_op jit(solution)/shard_map/all_gather | solution.py:82
  261.0 47.3 %copy-start.9 = (bf16[512,128]{1,0:T(8,128)(2,1)S(1)}, bf16[512,128]{1,0:T(8,128)(2,1)}, u32[]{:S(2)}) copy-start(bf16[512,128]{1,0:T(8,128)(2,1)} %param.30) | copy-start | bytes 393220
  277.6 33.9 %copy-start.6 = (s32[8192]{0:T(1024)S(1)}, s32[8192]{0:T(1024)}, u32[]{:S(2)}) copy-start(s32[8192]{0:T(1024)} %param.20) | copy-start | bytes 98308
  277.6 34.0 %copy-start.7 = (s32[8192]{0:T(1024)S(1)}, s32[8192]{0:T(1024)}, u32[]{:S(2)}) copy-start(s32[8192]{0:T(1024)} %param.19) | copy-start | bytes 98308
  277.7 107.2 %all-gather.9.cloned.1.call-start = ((), (), s32[]{:S(2)}) async-start(), calls=%async_computation.4 | async-start | bytes 17301504 | tf_op jit(solution)/shard_map/all_gather | solution.py:88
  311.5 1.0 copy-start.1
  311.5 203.7 %all-gather.11.cloned.1.call-start = ((), (), s32[]{:S(2)}) async-start(), calls=%async_computation.5 | async-start | bytes 10485760 | tf_op jit(solution)/shard_map/all_gather | solution.py:92
  421.0 94.2 %copy-start.10 = (bf16[512,128]{1,0:T(8,128)(2,1)S(1)}, bf16[512,128]{1,0:T(8,128)(2,1)}, u32[]{:S(2)}) copy-start(bf16[512,128]{1,0:T(8,128)(2,1)} %param.31) | copy-start | bytes 393220
Sparse Core Ops, SparseCore 0:
  9.7 89.5 all-gather.4
  277.8 30.4 all-gather.6
  311.6 73.1 all-gather.8
  428.5 86.5 all-gather.10
where the time goes:
time: 532 us; the launch traced here: 530 us
  waiting for transfers between devices  251 us (47%)
  local copies, waits for them, and re-layouts  139 us (26%)
  matrix products  95.2 us (18%)
  starting transfers between devices  14.9 us (3%)
  between operations  13.9 us (3%)
  other arithmetic  13.6 us (3%)
    all_gather x1, waiting for transfers between devices, local(): lax.all_gather(pair, 'mp', axis=1, tiled=True)  86.8 us
    all_gather x1, waiting for transfers between devices, local(): piece = lax.all_gather(edge_feats, 'mp', axis=1, tiled=True)  55.8 us
    all_gather x1, waiting for transfers between devices, local(): everything = lax.all_gather(atom_out, 'graph', axis=0, tiled=True)  48.3 us
    gather x1, local copies, waits for them, and re-layouts, local(): target_rows = jnp.take(everything, edge_target, axis=0)  36.2 us
    convert_element_type x1, local copies, waits for them, and re-layouts, local(): jnp.einsum('esb,esa->eba', weights, picked, preferred_element_type=jnp.fl...  35.4 us
    all_gather x1, waiting for transfers between devices, local(): lax.all_gather(atom_mid, 'mp', axis=1, tiled=True)  30.6 us
    all_to_all x1, waiting for transfers between devices, local(): lax.all_to_all(outgoing, 'graph', split_axis=0, concat_axis=0, tiled=True)  28.7 us
    dot_general x1, matrix products, local(): jnp.einsum('esb,esa->eba', weights, picked, preferred_element_type=jnp.fl...  26.9 us
  transfers between devices with their start and end apart: 6, of which 5 were waited for; matrix products, arithmetic and copies ran while one was open for 34% of the time, Pallas kernels for 0%

commit v1 on v0

v1 whole, which is shorter than its diff:
```python
import jax
import jax.numpy as jnp
from jax import lax
from jax.experimental import pallas as pl
from jax.experimental.pallas import tpu as pltpu
from jax.sharding import PartitionSpec as P

DT = 64
NB = 16
SLOTS = 8
CAP = 256
MP = 4
BF = jnp.bfloat16
F32 = jnp.float32


def triplet_kernel(down_ref, ids_ref, basis_ref, rep_ref, tile_ref, wbil_ref, out_ref):
    nblk = down_ref.shape[0]
    q = ids_ref.shape[0] // nblk
    weights = jnp.dot(basis_ref[...], tile_ref[...], preferred_element_type=F32)
    lanes = lax.broadcasted_iota(jnp.int32, (q, CAP), 1)
    for k in range(nblk):
        rows = slice(k * q, (k + 1) * q)
        table = jnp.dot(down_ref[k], rep_ref[...], preferred_element_type=F32).astype(BF)
        ids = ids_ref[rows, :]
        onehot = jnp.concatenate(
            [(ids[:, s : s + 1] == lanes).astype(F32).astype(BF) for s in range(SLOTS)], axis=0
        )
        bil = jnp.zeros((q, DT), F32)
        for j in range(4):
            cols = slice(256 * j, 256 * (j + 1))
            picked = jnp.dot(onehot, table[:, cols], preferred_element_type=F32)
            mixed = jnp.zeros((q, 256), F32)
            for s in range(SLOTS):
                w = weights[rows, 128 * s : 128 * (s + 1)]
                mixed = mixed + picked[s * q : (s + 1) * q] * jnp.concatenate([w, w], axis=1)
            bil = bil + jnp.dot(mixed.astype(BF), wbil_ref[cols, :], preferred_element_type=F32)
        out_ref[rows, :] = bil.astype(BF)


def triplets(down_all, ids, basis, w_bil):
    nblk = down_all.shape[0]
    rows = ids.shape[0]
    q = rows // nblk
    step = 4
    a = jnp.arange(NB * DT, dtype=jnp.int32)
    rep = (a[None, :] // NB == jnp.arange(DT, dtype=jnp.int32)[:, None]).astype(BF)
    src = (a // 128) * NB + a % NB
    tile = (src[None, :] == jnp.arange(128, dtype=jnp.int32)[:, None]).astype(BF)
    wperm = jnp.transpose(w_bil.reshape(NB, DT, DT), (1, 0, 2)).reshape(NB * DT, DT)
    return pl.pallas_call(
        triplet_kernel,
        grid=(nblk // step,),
        in_specs=[
            pl.BlockSpec((step, CAP, DT), lambda i: (i, 0, 0)),
            pl.BlockSpec((step * q, SLOTS), lambda i: (i, 0)),
            pl.BlockSpec((step * q, 128), lambda i: (i, 0)),
            pl.BlockSpec((DT, NB * DT), lambda i: (0, 0)),
            pl.BlockSpec((128, NB * DT), lambda i: (0, 0)),
            pl.BlockSpec((NB * DT, DT), lambda i: (0, 0)),
        ],
        out_specs=pl.BlockSpec((step * q, DT), lambda i: (i, 0)),
        out_shape=jax.ShapeDtypeStruct((rows, DT), BF),
        name="triplets",
    )(down_all, ids, basis, rep, tile, wperm)


def local(
    edge_feats,
    edge_source,
    edge_target,
    edge_live,
    trip_partner,
    trip_mask,
    trip_basis,
    atom_feats,
    w_msg,
    w_down,
    w_bil,
    w_up,
    w_atom,
    w_edge,
):
    n_edges = edge_feats.shape[0]
    width = edge_feats.shape[1]
    full = width * MP
    atoms_local = atom_feats.shape[0]
    blocks = n_edges // CAP
    q = CAP // MP
    rows = blocks * q
    m = lax.axis_index("mp")

    def quarter(v):
        return lax.dynamic_index_in_dim(
            v.reshape((blocks, MP, q) + v.shape[1:]), m, axis=1, keepdims=False
        )

    def gather_w(w):
        return lax.all_gather(w, "mp", axis=1, tiled=True)

    target_q = quarter(edge_target) % atoms_local
    source_q = (quarter(edge_source) % atoms_local).reshape(rows)
    live_q = quarter(edge_live).reshape(rows)
    in_ids = lax.all_to_all(target_q, "graph", split_axis=0, concat_axis=0, tiled=True).reshape(rows)

    pm = jnp.where(trip_mask != 0, trip_partner % CAP, -1)
    pm = lax.dynamic_index_in_dim(
        pm.reshape(SLOTS, blocks, MP, q), m, axis=2, keepdims=False
    ).reshape(SLOTS, rows)
    ids = jnp.transpose(pm)
    basis = quarter(trip_basis).reshape(rows, 128)

    x = lax.all_to_all(
        edge_feats.reshape(blocks, MP, q, width), "mp", split_axis=1, concat_axis=1, tiled=True
    )
    x = jnp.transpose(x, (0, 2, 1, 3)).reshape(rows, full)
    w_msg_f = gather_w(w_msg)
    w_up_f = gather_w(w_up)
    down = jnp.dot(x, w_down, preferred_element_type=F32).astype(BF)
    down_all = lax.all_gather(down.reshape(blocks, q, DT), "mp", axis=1, tiled=True)
    hid = jnp.dot(x, w_msg_f, preferred_element_type=F32)
    message = x.astype(F32) + jax.nn.silu(hid)
    bil = triplets(down_all, ids, basis, w_bil)
    total = message + jnp.dot(bil, w_up_f, preferred_element_type=F32)
    outgoing = (total * live_q.astype(F32)[:, None]).astype(BF)
    incoming = lax.all_to_all(
        outgoing.reshape(blocks, q, full), "graph", split_axis=0, concat_axis=0, tiled=True
    ).reshape(rows, full)
    atom_ids = jnp.arange(atoms_local, dtype=jnp.int32)
    onehot_in = (atom_ids[:, None] == in_ids[None, :]).astype(BF)
    partial = jnp.dot(onehot_in, incoming, preferred_element_type=F32).astype(BF)
    quarter_atoms = atoms_local // MP
    parts = lax.all_to_all(
        partial.reshape(MP, quarter_atoms, full), "mp", split_axis=0, concat_axis=0, tiled=True
    )
    arow = lax.all_to_all(
        atom_feats.reshape(MP, quarter_atoms, width), "mp", split_axis=0, concat_axis=0, tiled=True
    )
    arow = jnp.transpose(arow, (1, 0, 2)).reshape(quarter_atoms, full)
    atom_mid = (arow.astype(F32) + jnp.sum(parts.astype(F32), axis=0)).astype(BF)
    ahid = jnp.dot(atom_mid, gather_w(w_atom), preferred_element_type=F32)
    atom_rows = (atom_mid.astype(F32) + jax.nn.silu(ahid)).astype(BF)
    atom_full = lax.all_gather(atom_rows, "mp", axis=0, tiled=True)
    atom_out = lax.dynamic_slice_in_dim(atom_full, m * width, width, axis=1)

    onehot_t = (in_ids[:, None] == atom_ids[None, :]).astype(BF)
    target_rows = jnp.dot(onehot_t, atom_full, preferred_element_type=F32).astype(BF)
    target_rows = lax.all_to_all(
        target_rows.reshape(blocks, q, full), "graph", split_axis=0, concat_axis=0, tiled=True
    ).reshape(rows, full)
    onehot_s = (source_q[:, None] == atom_ids[None, :]).astype(BF)
    source_rows = jnp.dot(onehot_s, atom_full, preferred_element_type=F32)
    pair = (source_rows * target_rows.astype(F32)).astype(BF)
    ehid = jnp.dot(pair, gather_w(w_edge), preferred_element_type=F32)
    edge_rows = (total + jax.nn.silu(ehid)).astype(BF)
    back = jnp.transpose(edge_rows.reshape(blocks, q, MP, width), (0, 2, 1, 3))
    edge_out = lax.all_to_all(back, "mp", split_axis=1, concat_axis=1, tiled=True)
    return (edge_out.reshape(n_edges, width), atom_out)


def solution(mesh):
    return jax.shard_map(
        local,
        mesh=mesh,
        in_specs=(
            P("graph", "mp"),
            P("graph"),
            P("graph"),
            P("graph"),
            P(None, "graph"),
            P(None, "graph"),
            P("graph", None),
            P("graph", "mp"),
            P(None, "mp"),
            P(),
            P(),
            P(None, "mp"),
            P(None, "mp"),
            P(None, "mp"),
        ),
        out_specs=(P("graph", "mp"), P("graph", "mp")),
        check_vma=False,
    )
```

time: 532 us -> 371 us (0.70)
  waiting for transfers between devices: 251 us -> 122 us
  local copies, waits for them, and re-layouts: 139 us -> 26.8 us
  blocking collectives: 0 us -> 93.8 us
  matrix products: 95.2 us -> 37.6 us
  Pallas kernels: 0 us -> 34.2 us
  starting transfers between devices: 14.9 us -> 36.4 us
  other arithmetic: 13.6 us -> 5.04 us
    all_gather x4 -> x2, waiting for transfers between devices: 221 us -> 28.3 us  [the longest x1 28.3 us: local(): atom_full = lax.all_gather(atom_rows, 'mp', axis=0, tiled=True)]
    all_to_all x2 -> x6, waiting for transfers between devices: 28.7 us -> 93.2 us  [the longest x1 27.6 us: local(): lax.all_to_all(outgoing.reshape(blocks, q, full), 'graph', split_axis=0,...]
    all_gather x0 -> x4, blocking collectives: none -> 64 us  [gather_w(): return lax.all_gather(w, 'mp', axis=1, tiled=True)]
    gather x2 -> x0, local copies, waits for them, and re-layouts: 60.2 us -> none  [the longest x1 36.2 us: local(): target_rows = jnp.take(everything, edge_target, axis=0)]
    dot_general x14 -> x7, matrix products: 95.2 us -> 37.6 us  [the longest x1 9.97 us: local(): ehid = jnp.dot(pair, gather_w(w_edge), preferred_element_type=F32)]
    convert_element_type x1 -> x2, local copies, waits for them, and re-layouts: 35.4 us -> 1.07 us  [the longest x1 1 us: local(): down = jnp.dot(x, w_down, preferred_element_type=F32).astype(BF)]
    pallas_call x0 -> x1, Pallas kernels: none -> 34.2 us  [triplets(): pl.pallas_call(triplet_kernel, grid=(nblk // step,), in_specs=[pl.BlockSp...]
    all_to_all x0 -> x1, blocking collectives: none -> 29.8 us  [local(): lax.all_to_all(partial.reshape(MP, quarter_atoms, full), 'mp', split_axis...]
  transfers between devices with their start and end apart: 6 -> 8, of which waited for: 5 -> 5; matrix products, arithmetic and copies ran while one was open for 34% -> 7% of each run, Pallas kernels for 0% -> 9%
where the time goes in v1:
time: 371 us; the launch traced here: 370 us
  waiting for transfers between devices  122 us (33%)
  blocking collectives  93.8 us (25%)
  matrix products  37.6 us (10%)
  starting transfers between devices  36.4 us (10%)
  Pallas kernels  34.2 us (9%)
  local copies, waits for them, and re-layouts  26.8 us (7%)
  between operations  14.3 us (4%)
  other arithmetic  5.04 us (1%)
    all_gather x4, blocking collectives, gather_w(): return lax.all_gather(w, 'mp', axis=1, tiled=True)  64 us
    pallas_call x1, Pallas kernels, triplets(): pl.pallas_call(triplet_kernel, grid=(nblk // step,), in_specs=[pl.BlockSp...  34.2 us
    all_to_all x1, blocking collectives, local(): lax.all_to_all(partial.reshape(MP, quarter_atoms, full), 'mp', split_axis...  29.8 us
    all_gather x1, waiting for transfers between devices, local(): atom_full = lax.all_gather(atom_rows, 'mp', axis=0, tiled=True)  28.3 us
    all_to_all x1, waiting for transfers between devices, local(): lax.all_to_all(outgoing.reshape(blocks, q, full), 'graph', split_axis=0,...  27.6 us
    all_to_all x1, waiting for transfers between devices, local(): lax.all_to_all(edge_feats.reshape(blocks, MP, q, width), 'mp', split_axis...  25.9 us
    all_to_all x1, waiting for transfers between devices, local(): lax.all_to_all(back, 'mp', split_axis=1, concat_axis=1, tiled=True)  24.6 us
    all_to_all x1, waiting for transfers between devices, local(): lax.all_to_all(target_rows.reshape(blocks, q, full), 'graph', split_axis=...  15 us
  transfers between devices with their start and end apart: 8, of which 5 were waited for; matrix products, arithmetic and copies ran while one was open for 7% of the time, Pallas kernels for 9%

profile of v1, /device:TPU:0, one launch (start us, length us, event | category | flops | bytes accessed | tf_op | source)
XLA Modules:
  0.0 369.6 jit_solution(10318606841271711398)
XLA Ops:
  7.2 0.0 copy-start
  7.2 3.3 copy.30
  10.5 5.5 %all-to-all-start = ((bf16[32,4,64,128]{3,2,0,1:T(8,128)(2,1)}), bf16[32,4,64,128]{3,2,0,1:T(8,128)(2,1)}, u32[]{:S(2)}, u32[]{:S(2)}) async-start(bf16[32,4,64,128]{3,2,0,1:T(8,128)(2,1)} %copy.30), calls=%async_computation | async-start | bytes 4194304 | tf_op jit(solution)/shard_map/all_to_all | solution.py:113
  16.0 0.1 reshape.172
  16.1 0.7 and_select_fusion
  16.8 25.9 %all-to-all-done = bf16[32,4,64,128]{3,2,0,1:T(8,128)(2,1)} async-done(((bf16[32,4,64,128]{3,2,0,1:T(8,128)(2,1)}), bf16[32,4,64,128]{3,2,0,1:T(8,128)(2,1)}, u32[]{:S(2)}, u32[]{:S(2)}) %all-to-all-start) | async-done | bytes 2097184 | tf_op jit(solution)/shard_map/all_to_all | solution.py:113
  42.7 7.3 %all-to-all-start.2 = ((s32[32,1,64]{2,1,0:T(1,128)}), s32[32,1,64]{2,1,0:T(1,128)S(1)}, u32[]{:S(2)}, u32[]{:S(2)}) async-start(s32[32,1,64]{2,1,0:T(1,128)} %and_select_fusion), calls=%async_computation.2 | async-start | bytes 32768 | tf_op jit(solution)/shard_map/all_to_all | solution.py:104
  50.0 0.0 all-gather.3.cloned.1.call-start
  50.0 0.0 copy-start.13
  50.0 3.6 copy.31
  53.6 0.0 copy-start.1
  53.6 1.3 copy-done.1
  55.0 0.8 convolution_convert_fusion
  55.7 1.0 copy.32
  56.7 0.0 all-gather.3.cloned.1.call-update
  56.8 0.0 copy-start.10
  56.8 0.0 copy-start.12
  56.8 0.1 fusion.18
  56.9 0.0 copy-start.6
  56.9 0.3 reshape.164
  57.3 0.1 constant_dynamic-slice_fusion.2
  57.4 1.3 copy.39
  58.8 0.2 reshape.168
  59.0 1.1 copy.35
  60.1 0.1 reshape.173
  60.2 0.1 convert_reduce_fusion.1
  60.2 0.1 convert_element_type.75
  60.3 10.8 %all_gather.20 = bf16[64,512]{1,0:T(8,128)(2,1)S(1)} all-gather(bf16[64,128]{1,0:T(8,128)(2,1)S(1)} %copy-done.12), channel_id=1, replica_groups=mesh['graph'=32,'mp'=4] {'mp'}, dimensions={1}, use_global_device_ids=true | all-gather | bytes 81920 | tf_op jit(solution)/shard_map/all_gather | solution.py:99
  71.1 0.9 constant_dynamic-slice_fusion.1
  71.9 21.3 %all_gather.18 = bf16[512,512]{1,0:T(8,128)(2,1)S(1)} all-gather(bf16[512,128]{1,0:T(8,128)(2,1)S(1)} %copy-done.6), channel_id=1, replica_groups=mesh['graph'=32,'mp'=4] {'mp'}, dimensions={1}, use_global_device_ids=true | all-gather | bytes 655360 | tf_op jit(solution)/shard_map/all_gather | solution.py:99
  93.2 0.7 fusion.19.rep_ref
  93.9 0.8 fusion.16.tile_ref
  94.7 3.2 fusion.10
  97.9 34.2 %triplets.1 = bf16[2048,64]{1,0:T(8,128)(2,1)} custom-call(bf16[32,256,64]{2,1,0:T(8,128)(2,1)} %all-gather.3.cloned.1.call-done.down_ref, s32[2048,8]{1,0:T(8,128)} %bitcast.61, bf16[2048,128]{1,0:T(8,128)(2,1)} %bitcast.62, bf16[64,1024]{1,0:T(8,128)(2,1)} %fusion.19.rep_ref, bf16[128,1024]{1,0:T(8,128)(2,1)} %fusion.16.tile_ref, bf16[1024,64]{1,0:T(8,128)(2,1)} %bitcast.69), custom_call_target="tpu_custom_call" | custom-call | tf_op jit(solution)/shard_map/triplets/pallas_call | solution.py:51
  132.1 7.2 %multiply_convert_fusion = (bf16[2048,512]{1,0:T(8,128)(2,1)}, f32[2048,512]{1,0:T(8,128)}) fusion(f32[2048]{0:T(1024)S(1)} %convert_element_type.75, bf16[2048,64]{1,0:T(8,128)(2,1)} %triplets.1, bf16[64,512]{1,0:T(8,128)(2,1)S(1)} %all_gather.20, f32[2048,512]{1,0:T(8,128)} %fusion.10, bf16[256,8,4,128]{3,2,1,0:T(4,128)(2,1)} %bitcast.58), kind=kOutput, calls=%fused_computation.13 | convolution fusion | flops 143654912 | bytes 12918784 | tf_op jit(solution)/shard_map/dot_general | solution.py:124
  139.3 7.5 %all-to-all-start.3 = ((bf16[32,64,512]{2,1,0:T(8,128)(2,1)}), bf16[32,64,512]{2,1,0:T(8,128)(2,1)}, u32[]{:S(2)}, u32[]{:S(2)}) async-start(bf16[32,64,512]{2,1,0:T(8,128)(2,1)} %bitcast.64), calls=%async_computation.3 | async-start | bytes 4194304 | tf_op jit(solution)/shard_map/all_to_all | solution.py:126
  146.8 0.5 broadcast.145
  147.3 0.7 reduce.11
  148.0 0.1 eq.84
  148.1 27.6 %all-to-all-done.3 = bf16[32,64,512]{2,1,0:T(8,128)(2,1)} async-done(((bf16[32,64,512]{2,1,0:T(8,128)(2,1)}), bf16[32,64,512]{2,1,0:T(8,128)(2,1)}, u32[]{:S(2)}, u32[]{:S(2)}) %all-to-all-start.3) | async-done | bytes 2097184 | tf_op jit(solution)/shard_map/all_to_all | solution.py:126
  175.7 6.3 %fusion.8 = bf16[2048,512]{1,0:T(8,128)(2,1)S(1)} fusion(bf16[2048,512]{1,0:T(8,128)(2,1)} %bitcast.12, s32[2048]{0:T(1024)S(1)} %eq.84), kind=kOutput, calls=%fused_computation.16 | convolution fusion | flops 4300210176 | bytes 4202496 | tf_op jit(solution)/shard_map/dot_general | solution.py:131
  182.0 0.0 copy-start.7
  182.0 29.8 %all_to_all.36 = bf16[4,512,512]{2,1,0:T(8,128)(2,1)} all-to-all(bf16[4,512,512]{2,1,0:T(8,128)(2,1)S(1)} %bitcast.67), channel_id=1, replica_groups=mesh['graph'=32,'mp'=4] {'mp'}, dimensions={0} | all-to-all | bytes 4194304 | tf_op jit(solution)/shard_map/all_to_all | solution.py:133
  211.8 4.1 %all-to-all-start.1 = ((bf16[4,512,128]{2,1,0:T(8,128)(2,1)}), bf16[4,512,128]{2,1,0:T(8,128)(2,1)}, u32[]{:S(2)}, u32[]{:S(2)}) async-start(bf16[4,512,128]{2,1,0:T(8,128)(2,1)} %bitcast.9), calls=%async_computation.1 | async-start | bytes 1048576 | tf_op jit(solution)/shard_map/all_to_all | solution.py:136
  216.0 0.0 all-gather.5.cloned.1.call-start
  216.0 18.3 %all_gather.21 = bf16[512,512]{1,0:T(8,128)(2,1)} all-gather(bf16[512,128]{1,0:T(8,128)(2,1)S(1)} %copy-done.7), channel_id=1, replica_groups=mesh['graph'=32,'mp'=4] {'mp'}, dimensions={1}, use_global_device_ids=true | all-gather | bytes 655360 | tf_op jit(solution)/shard_map/all_gather | solution.py:99
  234.4 2.0 convert_reduce_fusion
  236.4 2.9 add_convert_fusion.1
  239.3 0.0 all-gather.5.cloned.1.call-update
  239.3 28.3 %all-gather.5.cloned.1.call-done = bf16[2048,512]{1,0:T(8,128)(2,1)} async-done(((bf16[512,512]{1,0:T(8,128)(2,1)}), bf16[2048,512]{1,0:T(8,128)(2,1)}) %all-gather.5.cloned.1.call-update) | async-done | bytes 2097168 | tf_op jit(solution)/shard_map/all_gather | solution.py:143
  267.6 7.3 %fusion.7 = bf16[2048,512]{1,0:T(8,128)(2,1)} fusion(bf16[2048,512]{1,0:T(8,128)(2,1)} %all-gather.5.cloned.1.call-done, s32[2048]{0:T(1024)S(1)} %eq.84), kind=kOutput, calls=%fused_computation.15 | convolution fusion | flops 4300210176 | bytes 4202496 | tf_op jit(solution)/shard_map/dot_general | solution.py:147
  274.9 7.4 %all-to-all-start.5 = ((bf16[32,64,512]{2,1,0:T(8,128)(2,1)}), bf16[32,64,512]{2,1,0:T(8,128)(2,1)}, u32[]{:S(2)}, u32[]{:S(2)}) async-start(bf16[32,64,512]{2,1,0:T(8,128)(2,1)} %bitcast.66), calls=%async_computation.5 | async-start | bytes 4194304 | tf_op jit(solution)/shard_map/all_to_all | solution.py:148
  282.3 0.1 reshape.170
  282.4 0.1 dynamic-slice_reduce_fusion
  282.4 0.1 squeeze.10
  282.5 13.6 %all_gather.23 = bf16[512,512]{1,0:T(8,128)(2,1)S(1)} all-gather(bf16[512,128]{1,0:T(8,128)(2,1)S(1)} %copy-done.8), channel_id=1, replica_groups=mesh['graph'=32,'mp'=4] {'mp'}, dimensions={1}, use_global_device_ids=true | all-gather | bytes 655360 | tf_op jit(solution)/shard_map/all_gather | solution.py:99
  296.1 15.0 %all-to-all-done.5 = bf16[32,64,512]{2,1,0:T(8,128)(2,1)} async-done(((bf16[32,64,512]{2,1,0:T(8,128)(2,1)}), bf16[32,64,512]{2,1,0:T(8,128)(2,1)}, u32[]{:S(2)}, u32[]{:S(2)}) %all-to-all-start.5) | async-done | bytes 2097184 | tf_op jit(solution)/shard_map/all_to_all | solution.py:148
  311.2 10.0 %add_convert_fusion = bf16[2048,512]{1,0:T(8,128)(2,1)} fusion(f32[2048,512]{1,0:T(8,128)} %get-tuple-element.3, bf16[512,512]{1,0:T(8,128)(2,1)S(1)} %all_gather.23, bf16[2048,512]{1,0:T(8,128)(2,1)} %bitcast.20, bf16[2048,512]{1,0:T(8,128)(2,1)} %all-gather.5.cloned.1.call-done, s32[2048]{0:T(1024)S(1)} %add_select_fusion.1), kind=kOutput, calls=%fused_computation.11 | convolution fusion | flops 5382340608 | bytes 11018240 | tf_op jit(solution)/shard_map/dot_general | solution.py:154
  321.1 4.0 %reshape.178 = bf16[32,64,4,128]{3,2,1,0:T(4,128)(2,1)} reshape(bf16[2048,512]{1,0:T(8,128)(2,1)} %add_convert_fusion) | data formatting | bytes 4194304 | tf_op jit(solution)/shard_map/reshape | solution.py:156
  325.1 3.5 copy.58
  328.6 4.5 %all-to-all-start.6 = ((bf16[32,4,64,128]{3,2,0,1:T(8,128)(2,1)}), bf16[32,4,64,128]{3,2,0,1:T(8,128)(2,1)}, u32[]{:S(2)}, u32[]{:S(2)}) async-start(bf16[32,4,64,128]{3,2,0,1:T(8,128)(2,1)} %bitcast.60), calls=%async_computation.6 | async-start | bytes 4194304 | tf_op jit(solution)/shard_map/all_to_all | solution.py:157
  333.1 1.9 constant_dynamic-slice_fusion
  334.9 24.6 %all-to-all-done.6 = bf16[32,4,64,128]{3,2,0,1:T(8,128)(2,1)} async-done(((bf16[32,4,64,128]{3,2,0,1:T(8,128)(2,1)}), bf16[32,4,64,128]{3,2,0,1:T(8,128)(2,1)}, u32[]{:S(2)}, u32[]{:S(2)}) %all-to-all-start.6) | async-done | bytes 2097184 | tf_op jit(solution)/shard_map/all_to_all | solution.py:157
  359.6 3.2 copy.38
  (26 shorter events, 0.1 us)
Async XLA Ops:
  7.2 63.9 %copy-start = (bf16[8192,128]{1,0:T(8,128)(2,1)S(1)}, bf16[8192,128]{1,0:T(8,128)(2,1)}, u32[]{:S(2)}) copy-start(bf16[8192,128]{1,0:T(8,128)(2,1)} %param.20) | copy-start | bytes 6291460
  10.5 5.6 %copy-start.9 = (s32[8192]{0:T(1024)S(1)}, s32[8192]{0:T(1024)}, u32[]{:S(2)}) copy-start(s32[8192]{0:T(1024)} %param.16) | copy-start | bytes 98308
  10.5 32.2 %all-to-all-start = ((bf16[32,4,64,128]{3,2,0,1:T(8,128)(2,1)}), bf16[32,4,64,128]{3,2,0,1:T(8,128)(2,1)}, u32[]{:S(2)}, u32[]{:S(2)}) async-start(bf16[32,4,64,128]{3,2,0,1:T(8,128)(2,1)} %copy.30), calls=%async_computation | async-start | bytes 4194304 | tf_op jit(solution)/shard_map/all_to_all | solution.py:113
  42.7 96.7 %all-to-all-start.2 = ((s32[32,1,64]{2,1,0:T(1,128)}), s32[32,1,64]{2,1,0:T(1,128)S(1)}, u32[]{:S(2)}, u32[]{:S(2)}) async-start(s32[32,1,64]{2,1,0:T(1,128)} %and_select_fusion), calls=%async_computation.2 | async-start | bytes 32768 | tf_op jit(solution)/shard_map/all_to_all | solution.py:104
  50.0 47.9 %all-gather.3.cloned.1.call-start = ((), (), s32[]{:S(2)}) async-start(), calls=%async_computation.7 | async-start | bytes 2621440 | tf_op jit(solution)/shard_map/all_gather | solution.py:120
  50.0 4.9 %copy-start.13 = (bf16[512,64]{0,1:T(8,128)(2,1)S(1)}, bf16[512,64]{0,1:T(8,128)(2,1)}, u32[]{:S(2)}) copy-start(bf16[512,64]{0,1:T(8,128)(2,1)} %param.23) | copy-start | bytes 196612
  53.6 1.3 copy-start.1
  55.0 1.8 copy-start.3
  55.0 1.8 copy-start.4
  55.7 3.1 copy-start.5
  56.8 3.3 copy-start.10
  56.8 3.5 copy-start.12
  56.9 15.0 %copy-start.6 = (bf16[512,128]{1,0:T(8,128)(2,1)S(1)}, bf16[512,128]{1,0:T(8,128)(2,1)}, u32[]{:S(2)}) copy-start(bf16[512,128]{1,0:T(8,128)(2,1)} %param.22) | copy-start | bytes 393220
  60.3 34.4 %copy-start.2 = (bf16[32,64,4,128]{3,2,1,0:T(4,128)(2,1)S(1)}, bf16[32,64,4,128]{3,2,1,0:T(4,128)(2,1)}, u32[]{:S(2)}) copy-start(bf16[32,64,4,128]{3,2,1,0:T(4,128)(2,1)} %copy-done.1) | copy-start | bytes 6291460
  139.3 36.4 %all-to-all-start.3 = ((bf16[32,64,512]{2,1,0:T(8,128)(2,1)}), bf16[32,64,512]{2,1,0:T(8,128)(2,1)}, u32[]{:S(2)}, u32[]{:S(2)}) async-start(bf16[32,64,512]{2,1,0:T(8,128)(2,1)} %bitcast.64), calls=%async_computation.3 | async-start | bytes 4194304 | tf_op jit(solution)/shard_map/all_to_all | solution.py:126
  182.0 34.0 %copy-start.7 = (bf16[512,128]{1,0:T(8,128)(2,1)S(1)}, bf16[512,128]{1,0:T(8,128)(2,1)}, u32[]{:S(2)}) copy-start(bf16[512,128]{1,0:T(8,128)(2,1)} %param.26) | copy-start | bytes 393220
  211.8 24.6 %all-to-all-start.1 = ((bf16[4,512,128]{2,1,0:T(8,128)(2,1)}), bf16[4,512,128]{2,1,0:T(8,128)(2,1)}, u32[]{:S(2)}, u32[]{:S(2)}) async-start(bf16[4,512,128]{2,1,0:T(8,128)(2,1)} %bitcast.9), calls=%async_computation.1 | async-start | bytes 1048576 | tf_op jit(solution)/shard_map/all_to_all | solution.py:136
  216.0 51.6 %all-gather.5.cloned.1.call-start = ((), (), s32[]{:S(2)}) async-start(), calls=%async_computation.8 | async-start | bytes 2621440 | tf_op jit(solution)/shard_map/all_gather | solution.py:143
  274.9 7.4 %copy-start.11 = (s32[8192]{0:T(1024)S(1)}, s32[8192]{0:T(1024)}, u32[]{:S(2)}) copy-start(s32[8192]{0:T(1024)} %param.15) | copy-start | bytes 98308
  274.9 7.6 %copy-start.8 = (bf16[512,128]{1,0:T(8,128)(2,1)S(1)}, bf16[512,128]{1,0:T(8,128)(2,1)}, u32[]{:S(2)}) copy-start(bf16[512,128]{1,0:T(8,128)(2,1)} %param.27) | copy-start | bytes 393220
  274.9 36.3 %all-to-all-start.5 = ((bf16[32,64,512]{2,1,0:T(8,128)(2,1)}), bf16[32,64,512]{2,1,0:T(8,128)(2,1)}, u32[]{:S(2)}, u32[]{:S(2)}) async-start(bf16[32,64,512]{2,1,0:T(8,128)(2,1)} %bitcast.66), calls=%async_computation.5 | async-start | bytes 4194304 | tf_op jit(solution)/shard_map/all_to_all | solution.py:148
  328.6 31.0 %all-to-all-start.6 = ((bf16[32,4,64,128]{3,2,0,1:T(8,128)(2,1)}), bf16[32,4,64,128]{3,2,0,1:T(8,128)(2,1)}, u32[]{:S(2)}, u32[]{:S(2)}) async-start(bf16[32,4,64,128]{3,2,0,1:T(8,128)(2,1)} %bitcast.60), calls=%async_computation.6 | async-start | bytes 4194304 | tf_op jit(solution)/shard_map/all_to_all | solution.py:157
Sparse Core Ops, SparseCore 0:
  56.9 38.9 all-gather.2
  239.4 28.1 all-gather.4

commit v2 on v0

v2 whole, which is shorter than its diff:
```python
import jax
import jax.numpy as jnp
from jax import lax
from jax.experimental import pallas as pl
from jax.experimental.pallas import tpu as pltpu
from jax.sharding import PartitionSpec as P

DT = 64
NB = 16
SLOTS = 8
CAP = 256
MP = 4
Q = CAP // MP
NG = 32
BLK = 8
D = 512
W = D // MP
ORDER = (2, 1, 3, 0)
BF = jnp.bfloat16
F32 = jnp.float32
MESH = pl.DeviceIdType.MESH


def silu(v):
    h = 0.5 * v
    return h + h * jnp.tanh(h)


def dot(a, b):
    return jnp.dot(a, b, preferred_element_type=F32)


def lanes_at(k, n):
    return pl.ds(pl.multiple_of(k * n, n), n)


def rows_at(k, n):
    return pl.ds(pl.multiple_of(k * n, n), n)


def enter(g, m, over_graph):
    sem = pltpu.get_barrier_semaphore()
    peers = [(g, (m + k) % MP) for k in range(1, MP)]
    if over_graph:
        peers += [((g + k) % NG, m) for k in range(1, NG)]
    for peer in peers:
        pl.semaphore_signal(sem, inc=1, device_id=peer, device_id_type=MESH)
    pl.semaphore_wait(sem, len(peers))


def remote(src, dst, send, recv, peer):
    return pltpu.make_async_remote_copy(
        src_ref=src, dst_ref=dst, send_sem=send, recv_sem=recv, device_id=peer, device_id_type=MESH
    )


def low_lanes(shape):
    return lax.broadcasted_iota(jnp.int32, shape, len(shape) - 1) < Q


def pair_row(ref, blk, m):
    half = m // 2
    a = ref[pl.ds(2 * blk + half, 1), :]
    b = ref[pl.ds(2 * blk + 2 + half, 1), :]
    odd = m % 2 == 1
    ra, rb = pltpu.roll(a, Q, 1), pltpu.roll(b, Q, 1)
    return jnp.where(low_lanes(a.shape), jnp.where(odd, ra, a), jnp.where(odd, b, rb))


def column(row):
    return jnp.transpose(jnp.broadcast_to(row.astype(F32), (128, 128)))


def message_kernel(
    ef,
    target,
    live,
    partner,
    mask,
    basis,
    w_msg,
    w_down,
    l_mat,
    w_up,
    w_atom,
    w_edge,
    af,
    total,
    incoming,
    in_ids,
    atom_f,
    edge_f,
    arow,
    x,
    dall,
    at,
    wrow,
    outg,
    idq,
    msg_f,
    up_f,
    zs,
    zr,
    zl,
    xs,
    xr,
    xl,
):
    g = lax.axis_index("graph")
    m = lax.axis_index("mp")
    enter(g, m, True)
    quarter_atoms = arow.shape[0]
    own = lanes_at(m, W)

    def group(c):
        return (g // BLK + c) % 4

    def blocks_of(c):
        return pl.ds(pl.multiple_of(group(c) * BLK, BLK), BLK)

    def exchange(kind, src_of, dst):
        for j in (2, 1, 3):
            t = (m + j) % MP
            remote(src_of(t), dst, zs.at[kind, j], zr.at[kind, j], (g, t)).start()

    def local(kind, src, dst):
        pltpu.make_async_copy(src, dst, zl.at[kind]).start()

    def moves(kind):
        if kind < 4:
            b = blocks_of(ORDER[kind])
            return (lambda t: ef.at[b, t]), x.at[b, :, own], ef.at[b, m]
        if kind < 8:
            p = pl.ds(pl.multiple_of(group(ORDER[kind - 4]) * 4, 4), 4)
            d = dall.at[p, rows_at(m, Q), :]
            return (lambda t: d), d, None
        if kind == 12:
            return (
                (lambda t: af.at[t]),
                arow.at[:, own],
                af.at[m],
            )
        src, dst = ((w_msg, msg_f), (w_up, up_f), (w_atom, atom_f), (w_edge, edge_f))[kind - 8]
        return (lambda t: src), dst.at[:, own], src

    def start(kind):
        src_of, dst, here = moves(kind)
        if here is not None:
            local(kind, here, dst)
        exchange(kind, src_of, dst)

    def arrived(kind):
        src_of, dst, here = moves(kind)
        if here is not None:
            pltpu.make_async_copy(here, dst, zl.at[kind]).wait()
        for j in (2, 1, 3):
            t = (m + j) % MP
            remote(src_of(t), dst, zs.at[kind, j], zr.at[kind, j], (g, t)).wait_recv()

    def sent(kind):
        src_of, dst, here = moves(kind)
        for j in (2, 1, 3):
            t = (m + j) % MP
            remote(src_of(t), dst, zs.at[kind, j], zr.at[kind, j], (g, t)).wait_send()

    start(0)
    start(8)
    start(9)
    start(1)

    def write_ids(p, carry):
        row = pair_row(target, 2 * p, m) & 2047
        idq[2 * p] = row
        idq[2 * p + 1] = pltpu.roll(row, Q, 1)
        return carry

    lax.fori_loop(0, NG // 2, write_ids, 0)

    def weights_of(blk0):
        t = jnp.transpose(
            jnp.concatenate([basis[blk0, m], basis[blk0 + 1, m]], axis=0).astype(F32)
        ).reshape(SLOTS, 2, 8, 128)
        lo, hi = t[:, 0], t[:, 1]
        low = low_lanes((SLOTS, 8, 128))
        return (
            jnp.where(low, lo, pltpu.roll(hi.reshape(64, 128), Q, 1).reshape(SLOTS, 8, 128)),
            jnp.where(low, pltpu.roll(lo.reshape(64, 128), Q, 1).reshape(SLOTS, 8, 128), hi),
        )

    def ids_of(blk):
        cols = lanes_at(2 * blk + m // 2, 128)
        v = jnp.where(mask[:, cols] != 0, partner[:, cols] & 255, -1)
        r = pltpu.roll(v, Q, 1)
        odd = m % 2 == 1
        low = low_lanes(v.shape)
        return jnp.where(low, jnp.where(odd, r, v), jnp.where(odd, v, r))

    def spread_pair(c, i):
        blk0 = group(c) * BLK + 2 * i
        both = weights_of(blk0)
        for half in range(2):
            blk = blk0 + half
            w = both[half]
            for s in range(SLOTS):
                for j in range(8):
                    wrow[s * 8 + j] = jnp.broadcast_to(w[s, j : j + 1, :], (16, 128)).astype(BF)
            ids = ids_of(blk)

            def part(pt, carry):
                p_ids = lax.broadcasted_iota(jnp.int32, (32, 128), 0) + 32 * pt
                acc = [jnp.zeros((2, 16, 128), BF) for _ in range(8)]
                for s in range(SLOTS):
                    hot = (
                        jnp.where(ids[s : s + 1, :] == p_ids, 1.0, 0.0).astype(BF).reshape(2, 16, 128)
                    )
                    for j in range(8):
                        acc[j] = acc[j] + hot * wrow[s * 8 + j][None]
                for j in range(8):
                    at[blk, rows_at(pt, 32), 128 * j : 128 * (j + 1)] = acc[j].reshape(32, 128)
                return carry

            lax.fori_loop(0, 8, part, 0)

    def spread(c):
        def body(i, carry):
            spread_pair(c, i)
            return carry

        lax.fori_loop(0, BLK // 2, body, 0)

    def down(c):
        def body(i, carry):
            blk0 = group(c) * BLK + 2 * i
            rows = x[pl.ds(blk0, 2)].reshape(128, D)
            d = dot(rows, w_down[...])
            dall[group(c) * 4 + i, rows_at(m, Q), :] = jnp.concatenate(
                [d[:Q], d[Q:]], axis=1
            ).astype(BF)
            return carry

        lax.fori_loop(0, BLK // 2, body, 0)

    def hidden(c):
        def body(i, carry):
            blk0 = group(c) * BLK + 2 * i
            rows = x[pl.ds(blk0, 2)].reshape(128, D)
            total[rows_at(group(c) * 4 + i, 128), :] = rows.astype(F32) + silu(
                dot(rows, msg_f[...])
            )
            return carry

        lax.fori_loop(0, BLK // 2, body, 0)

    def finish(c):
        def body(i, carry):
            p = group(c) * 4 + i
            blk0 = 2 * p
            dt = jnp.transpose(dall[p].astype(F32)).astype(BF)
            sides = []
            for half in range(2):
                mixed = dot(dt[half * DT : (half + 1) * DT], at[blk0 + half]).astype(BF)
                sides.append(
                    jnp.concatenate([mixed[:, 128 * j : 128 * (j + 1)] for j in range(8)], axis=0)
                )
            o = dot(l_mat[...], jnp.concatenate(sides, axis=1))
            a, b = o[:, :128], o[:, 128:]
            low = low_lanes((DT, 128))
            bil_t = jnp.where(
                low, a[:DT] + pltpu.roll(a[DT:], Q, 1), pltpu.roll(b[:DT], Q, 1) + b[DT:]
            )
            bil = jnp.transpose(bil_t).astype(BF)
            rows = rows_at(p, 128)
            tot = total[rows, :] + dot(bil, up_f[...])
            total[rows, :] = tot
            alive = column(pair_row(live, blk0, m))
            alive = jnp.concatenate([alive] * 4, axis=1)
            outg[pl.ds(blk0, 2)] = (tot * alive).astype(BF).reshape(2, Q, D)
            return carry

        lax.fori_loop(0, BLK // 2, body, 0)

    def block_copy(n, d):
        return remote(outg.at[d], incoming.at[g], xs.at[0, n], xr.at[0, g], (d, m))

    def ids_copy(n, d):
        return remote(idq.at[d], in_ids.at[g], xs.at[1, n], xr.at[1, g], (d, m))

    def others(c):
        if c == 0:
            return [(24 + k, group(c) * BLK + (g + k) % BLK) for k in range(1, BLK)]
        return [(8 * ORDER.index(c) + k, group(c) * BLK + k) for k in range(BLK)]

    def send(c):
        if c == 0:
            pltpu.make_async_copy(outg.at[g], incoming.at[g], xl.at[0]).start()
            pltpu.make_async_copy(idq.at[g], in_ids.at[g], xl.at[1]).start()
        for n, d in others(c):
            block_copy(n, d).start()
            ids_copy(n, d).start()

    spread(ORDER[0])
    spread(ORDER[1])
    arrived(0)
    down(ORDER[0])
    start(4)
    start(2)
    arrived(8)
    hidden(ORDER[0])
    spread(ORDER[2])
    arrived(1)
    down(ORDER[1])
    start(5)
    start(3)
    arrived(9)
    arrived(4)
    finish(ORDER[0])
    hidden(ORDER[1])
    send(ORDER[0])
    spread(ORDER[3])
    arrived(2)
    down(ORDER[2])
    start(6)
    arrived(5)
    finish(ORDER[1])
    hidden(ORDER[2])
    send(ORDER[1])
    arrived(3)
    down(ORDER[3])
    start(7)
    start(12)
    start(10)
    start(11)
    arrived(6)
    finish(ORDER[2])
    hidden(ORDER[3])
    send(ORDER[2])
    arrived(7)
    finish(ORDER[3])
    send(ORDER[3])
    for kind in (10, 11, 12):
        arrived(kind)
    for kind in range(13):
        sent(kind)
    pltpu.make_async_copy(outg.at[g], incoming.at[g], xl.at[0]).wait()
    pltpu.make_async_copy(idq.at[g], in_ids.at[g], xl.at[1]).wait()
    for k in range(1, NG):
        s = (g + k) % NG
        remote(outg.at[s], incoming.at[s], xs.at[0, 0], xr.at[0, s], (s, m)).wait_recv()
        remote(idq.at[s], in_ids.at[s], xs.at[1, 0], xr.at[1, s], (s, m)).wait_recv()
    for c in ORDER:
        for n, d in others(c):
            block_copy(n, d).wait_send()
            ids_copy(n, d).wait_send()


def atom_kernel(inc, ids, arow, atom_f, afull, aout, idr, pbuf, rbuf, own, hot, ps, pr, us, ur):
    g = lax.axis_index("graph")
    m = lax.axis_index("mp")
    enter(g, m, False)
    quarter = arow.shape[0]
    h2 = quarter // 2
    up, dn = (m + 1) % MP, (m + 3) % MP

    def pairs(i, carry):
        a, b = ids[2 * i], ids[2 * i + 1]
        idr[pl.ds(i, 1), :] = jnp.where(low_lanes(a.shape), a, pltpu.roll(b, Q, 1))
        return carry

    lax.fori_loop(0, NG // 2, pairs, 0)

    def part(j, h):
        base = ((m + j) % MP) * quarter + h * h2

        def build(i, carry):
            at = lax.broadcasted_iota(jnp.int32, (h2, 128), 0) + base
            hot[:, lanes_at(i, 128)] = jnp.where(idr[pl.ds(i, 1), :] == at, 1.0, 0.0).astype(BF)
            return carry

        lax.fori_loop(0, NG // 2, build, 0)
        return dot(hot[...], inc[...])

    def copy(j, h):
        t = (m + j) % MP
        rows = pl.ds(h * h2, h2)
        return remote(pbuf.at[j, rows], rbuf.at[j, rows], ps.at[j, h], pr.at[j, h], (g, t))

    waiting = None
    for j in ORDER:
        for h in range(2):
            v = part(j, h)
            if j == 0:
                own[h * h2 : (h + 1) * h2, :] = v + arow[h * h2 : (h + 1) * h2, :].astype(F32)
            else:
                pbuf[j, h * h2 : (h + 1) * h2, :] = v.astype(BF)
            if waiting is not None:
                copy(*waiting).start()
                waiting = None
            if j != 0:
                waiting = (j, h)

    def rows_of(src, h):
        return afull.at[pl.ds(pl.multiple_of(src * quarter + h * h2, h2), h2)]

    def own_copy(h, to):
        t = up if to == 0 else dn
        return remote(rows_of(m, h), rows_of(m, h), us.at[to, h], ur.at[to, h], (g, t))

    def relay(to):
        src, t = (dn, up) if to == 0 else (up, dn)
        return remote(rows_of(src, to), rows_of(src, to), us.at[2, to], ur.at[2, to], (g, t))

    for h in range(2):
        rows = slice(h * h2, (h + 1) * h2)
        for j in (2, 1, 3):
            copy(j, h).wait_recv()
        s = own[rows, :]
        for j in (1, 2, 3):
            s = s + rbuf[j, rows, :].astype(F32)
        mid = s.astype(BF)
        out = (mid.astype(F32) + silu(dot(mid, atom_f[...]))).astype(BF)
        afull[pl.ds(pl.multiple_of(m * quarter + h * h2, h2), h2), :] = out
        for to in (h, 1 - h):
            own_copy(h, to).start()
    own_copy(0, 0).wait_recv()
    relay(0).start()
    own_copy(1, 1).wait_recv()
    relay(1).start()
    own_copy(0, 1).wait_recv()
    own_copy(1, 0).wait_recv()
    relay(0).wait_recv()
    relay(1).wait_recv()
    aout[...] = afull[:, lanes_at(m, W)]
    for h in range(2):
        for j in (1, 2, 3):
            copy(j, h).wait_send()
        for to in range(2):
            own_copy(h, to).wait_send()
        relay(h).wait_send()


def edge_kernel(afull, ids, source, total, edge_f, out, hot, sbuf, tbuf, src, ebuf, xs, xr, xl, zs, zr, zl):
    g = lax.axis_index("graph")
    m = lax.axis_index("mp")
    enter(g, m, True)
    n_atoms = afull.shape[0]

    def group(c):
        return (g // BLK + c) % 4

    def pick(row_of):
        def build(i, carry):
            col = column(row_of(i))
            for k in range(n_atoms // 128):
                lane = lax.broadcasted_iota(jnp.int32, (128, 128), 1).astype(F32) + 128.0 * k
                hot[rows_at(i, 128), 128 * k : 128 * (k + 1)] = jnp.where(
                    col == lane, 1.0, 0.0
                ).astype(BF)
            return carry

        lax.fori_loop(0, BLK // 2, build, 0)
        return dot(hot[...], afull[...]).astype(BF).reshape(BLK, Q, D)

    def others(c):
        if c == 0:
            return [(24 + k, group(c) * BLK + (g + k) % BLK) for k in range(1, BLK)]
        return [(8 * ORDER.index(c) + k, group(c) * BLK + k) for k in range(BLK)]

    def block_copy(n, d):
        return remote(sbuf.at[d], tbuf.at[g], xs.at[n], xr.at[g], (d, m))

    def send(c):
        if c == 0:
            pltpu.make_async_copy(sbuf.at[g], tbuf.at[g], xl).start()
        for n, d in others(c):
            block_copy(n, d).start()

    def blocks_at(gr):
        return pl.ds(pl.multiple_of(gr * BLK, BLK), BLK)

    previous = None
    for c in ORDER:

        def row_of(i, c=c):
            blk0 = group(c) * BLK + 2 * i
            a, b = ids[blk0], ids[blk0 + 1]
            return jnp.where(low_lanes(a.shape), a, pltpu.roll(b, Q, 1))

        sbuf[blocks_at(group(c))] = pick(row_of)
        if previous is not None:
            send(previous)
        previous = c
    for n, c in enumerate(ORDER):

        def row_of(i, c=c):
            blk0 = group(-c) * BLK + 2 * i
            return pair_row(source, blk0, m) & 2047

        src[blocks_at(group(-c))] = pick(row_of)
        if n == 0:
            send(previous)

    def back(c, j):
        b = blocks_at(group(-c))
        t = (m + j) % MP
        n = ORDER.index(c)
        return remote(
            ebuf.at[b, :, lanes_at(t, W)], out.at[b, m], zs.at[n, j], zr.at[n, j], (g, t)
        )

    def here(c):
        b = blocks_at(group(-c))
        return pltpu.make_async_copy(ebuf.at[b, :, lanes_at(m, W)], out.at[b, m], zl.at[ORDER.index(c)])

    def push(c):
        here(c).start()
        for j in (2, 1, 3):
            back(c, j).start()

    previous = None
    for c in ORDER:
        gr = group(-c)
        if c == 0:
            pltpu.make_async_copy(sbuf.at[g], tbuf.at[g], xl).wait()
            sources = [gr * BLK + (g + k) % BLK for k in range(1, BLK)]
        else:
            sources = [gr * BLK + k for k in range(BLK)]
        for s in sources:
            remote(sbuf.at[s], tbuf.at[s], xs.at[0], xr.at[s], (s, m)).wait_recv()

        def body(i, carry, gr=gr):
            blk = pl.ds(gr * BLK + 2 * i, 2)
            pair = (
                src[blk].reshape(128, D).astype(F32) * tbuf[blk].reshape(128, D).astype(F32)
            ).astype(BF)
            v = total[rows_at(gr * 4 + i, 128), :] + silu(dot(pair, edge_f[...]))
            ebuf[blk] = v.astype(BF).reshape(2, Q, D)
            return carry

        lax.fori_loop(0, BLK // 2, body, 0)
        push(c)
    for c in ORDER:
        here(c).wait()
        for j in (2, 1, 3):
            back(c, j).wait()
        for n, d in others(c):
            block_copy(n, d).wait_send()


def vmem(shape, dtype):
    return pltpu.VMEM(shape, dtype)


def run(kernel, outs, scratch, cid, name, args):
    spec = pl.BlockSpec(memory_space=pltpu.VMEM)
    return pl.pallas_call(
        kernel,
        out_shape=tuple(jax.ShapeDtypeStruct(s, d) for s, d in outs),
        in_specs=[spec] * len(args),
        out_specs=tuple([spec] * len(outs)),
        scratch_shapes=scratch,
        compiler_params=pltpu.CompilerParams(
            collective_id=cid, has_side_effects=True, vmem_limit_bytes=56 << 20
        ),
        name=name,
    )(*args)


def local(
    edge_feats,
    edge_source,
    edge_target,
    edge_live,
    trip_partner,
    trip_mask,
    trip_basis,
    atom_feats,
    w_msg,
    w_down,
    w_bil,
    w_up,
    w_atom,
    w_edge,
):
    n_edges = edge_feats.shape[0]
    n_atoms = atom_feats.shape[0]
    rows = n_edges // MP
    quarter = n_atoms // MP
    dma = pltpu.SemaphoreType.DMA
    l_mat = jnp.transpose(jnp.concatenate([w_bil[: 8 * DT], w_bil[8 * DT :]], axis=1))
    total, incoming, in_ids, atom_f, edge_f, arow = run(
        message_kernel,
        [
            ((rows, D), F32),
            ((NG, Q, D), BF),
            ((NG, 1, 128), jnp.int32),
            ((D, D), BF),
            ((D, D), BF),
            ((quarter, D), BF),
        ],
        [
            vmem((NG, Q, D), BF),
            vmem((NG // 2, CAP, 128), BF),
            vmem((NG, CAP, NB * Q), BF),
            vmem((64, 16, 128), BF),
            vmem((NG, Q, D), BF),
            vmem((NG, 1, 128), jnp.int32),
            vmem((D, D), BF),
            vmem((DT, D), BF),
            dma((13, 4)),
            dma((13, 4)),
            dma((13,)),
            dma((2, NG)),
            dma((2, NG)),
            dma((2,)),
        ],
        0,
        "messages",
        (
            edge_feats.reshape(NG, MP, Q, W),
            edge_target.reshape(2 * NG, 128),
            edge_live.reshape(2 * NG, 128),
            trip_partner,
            trip_mask,
            trip_basis.reshape(NG, MP, Q, 128),
            w_msg,
            w_down,
            l_mat,
            w_up,
            w_atom,
            w_edge,
            atom_feats.reshape(MP, quarter, W),
        ),
    )
    afull, aout = run(
        atom_kernel,
        [((n_atoms, D), BF), ((n_atoms, W), BF)],
        [
            vmem((NG // 2, 128), jnp.int32),
            vmem((MP, quarter, D), BF),
            vmem((MP, quarter, D), BF),
            vmem((quarter, D), F32),
            vmem((quarter // 2, rows), BF),
            dma((4, 2)),
            dma((4, 2)),
            dma((3, 2)),
            dma((3, 2)),
        ],
        1,
        "atoms",
        (incoming.reshape(rows, D), in_ids, arow, atom_f),
    )
    (edge_out,) = run(
        edge_kernel,
        [((NG, MP, Q, W), BF)],
        [
            vmem((BLK * Q, n_atoms), BF),
            vmem((NG, Q, D), BF),
            vmem((NG, Q, D), BF),
            vmem((NG, Q, D), BF),
            vmem((NG, Q, D), BF),
            dma((NG,)),
            dma((NG,)),
            dma,
            dma((4, 4)),
            dma((4, 4)),
            dma((4,)),
        ],
        2,
        "edges",
        (afull, in_ids, edge_source.reshape(2 * NG, 128), total, edge_f),
    )
    return (edge_out.reshape(n_edges, W), aout)


def solution(mesh):
    return jax.shard_map(
        local,
        mesh=mesh,
        in_specs=(
            P("graph", "mp"),
            P("graph"),
            P("graph"),
            P("graph"),
            P(None, "graph"),
            P(None, "graph"),
            P("graph", None),
            P("graph", "mp"),
            P(None, "mp"),
            P(),
            P(),
            P(None, "mp"),
            P(None, "mp"),
            P(None, "mp"),
        ),
        out_specs=(P("graph", "mp"), P("graph", "mp")),
        check_vma=False,
    )
```

time: 532 us -> 210 us (0.39)
  the two profiles are of different devices: /device:TPU:0 before, /device:TPU:29 now
where the time goes in v2:
time: 210 us
  Pallas kernels  202 us (96%)
  local copies, waits for them, and re-layouts  6.38 us (3%)
    pallas_call x3, Pallas kernels, run(): pl.pallas_call(kernel, out_shape=tuple((jax.ShapeDtypeStruct(s, d) for s,...  202 us
    unnamed x5, local copies, waits for them, and re-layouts  5.5 us

profile of v2, /device:TPU:29, one launch (start us, length us, event | category | flops | bytes accessed | tf_op | source)
XLA Modules:
  0.0 209.8 jit_solution(8212951590221973629)
XLA Ops:
  0.6 1.6 copy.16.w_down
  2.2 0.9 fusion
  3.1 0.7 maximum_bitcast_fusion.l_mat
  3.8 80.2 %messages.1 = (f32[2048,512]{1,0:T(8,128)}, bf16[32,64,512]{2,1,0:T(8,128)(2,1)}, s32[32,1,128]{2,1,0:T(1,128)}, bf16[512,512]{1,0:T(8,128)(2,1)}, bf16[512,512]{1,0:T(8,128)(2,1)}, /*index=5*/bf16[512,512]{1,0:T(8,128)(2,1)}) custom-call(bf16[32,4,64,128]{3,2,1,0:T(8,128)(2,1)} %bitcast.11, s32[64,128]{1,0:T(8,128)} %bitcast.15, s32[64,128]{1,0:T(8,128)} %bitcast.16, ...), custom_call_target="tpu_custom_call" | custom-call | tf_op jit(solution)/shard_map/messages/pallas_call | solution.py:555
  84.0 51.5 %atoms.1 = (bf16[2048,512]{1,0:T(8,128)(2,1)}, bf16[2048,128]{1,0:T(8,128)(2,1)}) custom-call(bf16[2048,512]{1,0:T(8,128)(2,1)} %bitcast.13, s32[32,1,128]{2,1,0:T(1,128)} %get-tuple-element.11.ids, bf16[512,512]{1,0:T(8,128)(2,1)} %get-tuple-element.12.arow, bf16[512,512]{1,0:T(8,128)(2,1)} %get-tuple-element.13.atom_f), custom_call_target="tpu_custom_call" | custom-call | tf_op jit(solution)/shard_map/atoms/pallas_call | solution.py:555
  135.5 70.3 %edges.1 = bf16[32,4,64,128]{3,2,1,0:T(8,128)(2,1)} custom-call(bf16[2048,512]{1,0:T(8,128)(2,1)} %get-tuple-element.14.afull, s32[32,1,128]{2,1,0:T(1,128)} %get-tuple-element.11.ids, s32[64,128]{1,0:T(8,128)} %bitcast.17, f32[2048,512]{1,0:T(8,128)} %get-tuple-element.15.total, bf16[512,512]{1,0:T(8,128)(2,1)} %get-tuple-element.16.edge_f), custom_call_target="tpu_custom_call" | custom-call | tf_op jit(solution)/shard_map/edges/pallas_call | solution.py:555
  205.9 0.0 copy-start
  205.9 3.1 %copy.19 = bf16[8192,128]{1,0:T(8,128)(2,1)} copy(bf16[8192,128]{1,0:T(8,128)(2,1)} %bitcast.10) | data formatting | bytes 4194304
  209.0 0.0 copy-done
  209.0 0.8 copy.20
Async XLA Ops:
  205.9 3.1 %copy-start = (bf16[2048,128]{1,0:T(8,128)(2,1)S(1)}, bf16[2048,128]{1,0:T(8,128)(2,1)}, u32[]{:S(2)}) copy-start(bf16[2048,128]{1,0:T(8,128)(2,1)} %get-tuple-element.23) | copy-start | bytes 1572868

commit v3 on v0

v3 whole, which is shorter than its diff:
```python
import jax
import jax.numpy as jnp
from jax import lax
from jax.experimental import pallas as pl
from jax.experimental.pallas import tpu as pltpu
from jax.sharding import PartitionSpec as P

DT = 64
NB = 16
SLOTS = 8
CAP = 256
MP = 4
Q = CAP // MP
NG = 32
BLK = 8
D = 512
W = D // MP
ORDER = (1, 3, 0, 2)
NEAR = (2, 1, 3, 0)
BF = jnp.bfloat16
F32 = jnp.float32
MESH = pl.DeviceIdType.MESH


def silu(v):
    h = 0.5 * v
    return h + h * jnp.tanh(h)


def dot(a, b):
    return jnp.dot(a, b, preferred_element_type=F32)


def lanes_at(k, n):
    return pl.ds(pl.multiple_of(k * n, n), n)


def rows_at(k, n):
    return pl.ds(pl.multiple_of(k * n, n), n)


def enter(g, m, over_graph):
    sem = pltpu.get_barrier_semaphore()
    peers = [(g, (m + k) % MP) for k in range(1, MP)]
    if over_graph:
        peers += [((g + k) % NG, m) for k in range(1, NG)]
    for peer in peers:
        pl.semaphore_signal(sem, inc=1, device_id=peer, device_id_type=MESH)
    pl.semaphore_wait(sem, len(peers))


def remote(src, dst, send, recv, peer):
    return pltpu.make_async_remote_copy(
        src_ref=src, dst_ref=dst, send_sem=send, recv_sem=recv, device_id=peer, device_id_type=MESH
    )


def low_lanes(shape):
    return lax.broadcasted_iota(jnp.int32, shape, len(shape) - 1) < Q


def pair_row(ref, blk, m):
    half = m // 2
    a = ref[pl.ds(2 * blk + half, 1), :]
    b = ref[pl.ds(2 * blk + 2 + half, 1), :]
    odd = m % 2 == 1
    ra, rb = pltpu.roll(a, Q, 1), pltpu.roll(b, Q, 1)
    return jnp.where(low_lanes(a.shape), jnp.where(odd, ra, a), jnp.where(odd, b, rb))


def column(row):
    return jnp.transpose(jnp.broadcast_to(row.astype(F32), (128, 128)))


def block_kernel(
    ef,
    target,
    live,
    source,
    partner,
    mask,
    basis,
    w_msg,
    w_down_t,
    w_bil_t,
    w_up,
    w_atom,
    w_edge,
    af,
    out,
    aout,
    x,
    dall,
    at,
    wrow,
    mix,
    l_mat,
    total,
    outg,
    incoming,
    tbuf,
    idq,
    in_ids,
    idr,
    wf,
    up_f,
    hot,
    tmp,
    part_f,
    own,
    pbuf,
    rbuf,
    afull,
    srcb,
    es,
    er,
    el,
    ds,
    dr,
    ws,
    wr,
    wl,
    vs,
    vr,
    xs,
    xr,
    xl,
    ps,
    pr,
    us,
    ur,
    zs,
    zr,
    zl,
):
    g = lax.axis_index("graph")
    m = lax.axis_index("mp")
    cx, cy, core = g // 8, (g // 2) % 4, g % 2
    quarter = own.shape[0]
    h2 = quarter // 2
    n_atoms = afull.shape[0]
    up, dn, op = (m + 1) % MP, (m + 3) % MP, (m + 2) % MP

    def to_pair(k, i):
        return ((cx + i) % 4) * 4 + (cy + k - i + 4) % 4

    def from_pair(k, i):
        return ((cx - i + 4) % 4) * 4 + (cy - k + i + 4) % 4

    def two(p):
        return pl.ds(2 * p, 2)

    enter(g, m, True)

    def ef_copy(k, i, j):
        p, n = to_pair(k, i), 4 * k + i
        t = (m + j) % MP
        return remote(ef.at[two(p), t], x.at[m, two(p)], es.at[n, j], er.at[n, j], (g, t))

    def ef_here(k, i):
        p = to_pair(k, i)
        return pltpu.make_async_copy(ef.at[two(p), m], x.at[m, two(p)], el.at[4 * k + i])

    def ef_start(k):
        for i in range(4):
            ef_here(k, i).start()
            for j in (2, 1, 3):
                ef_copy(k, i, j).start()

    def ef_wait(k):
        for i in range(4):
            ef_here(k, i).wait()
            for j in (2, 1, 3):
                ef_copy(k, i, j).wait_recv()

    def down_copy(k, i, j):
        p, n = to_pair(k, i), 4 * k + i
        d = dall.at[p, rows_at(m, Q), :]
        return remote(d, d, ds.at[n, j], dr.at[n, j], (g, (m + j) % MP))

    def down_start(k):
        for i in range(4):
            for j in (2, 1, 3):
                down_copy(k, i, j).start()

    def down_wait(k):
        for i in range(4):
            for j in (2, 1, 3):
                down_copy(k, i, j).wait_recv()

    weights = (w_msg, w_atom, w_edge)
    piece = pl.ds(pl.multiple_of(16 * g, 16), 16)

    def w_copy(n, j):
        peer = (g, (m + j) % MP)
        if n == 3:
            return remote(w_up, up_f.at[m], ws.at[n, j], wr.at[n, j], peer)
        return remote(weights[n].at[piece], wf.at[n, m, piece], ws.at[n, j], wr.at[n, j], peer)

    def w_here(n):
        if n == 3:
            return pltpu.make_async_copy(w_up, up_f.at[m], wl.at[n])
        return pltpu.make_async_copy(weights[n].at[piece], wf.at[n, m, piece], wl.at[n])

    def w_spread(n, k):
        d = (g + k) % NG
        ref = wf.at[n, :, piece]
        return remote(ref, ref, vs.at[n, k], vr.at[n, g], (d, m))

    def w_spread_wait(n):
        for k in range(1, NG):
            s = (g + k) % NG
            ref = wf.at[n, :, pl.ds(pl.multiple_of(16 * s, 16), 16)]
            remote(ref, ref, vs.at[n, k], vr.at[n, s], (s, m)).wait_recv()

    def w_full(n):
        return jnp.concatenate([wf[n, j] for j in range(MP)], axis=1)

    for n in range(4):
        w_here(n).start()
        for j in (2, 1, 3):
            w_copy(n, j).start()
    ef_start(ORDER[0])
    ef_start(ORDER[1])

    def write_ids(p, carry):
        row = pair_row(target, 2 * p, m) & 2047
        idq[2 * p] = row
        idq[2 * p + 1] = pltpu.roll(row, Q, 1)
        return carry

    lax.fori_loop(0, NG // 2, write_ids, 0)
    l_mat[:DT, :] = w_bil_t[:, : 8 * DT]
    l_mat[DT:, :] = w_bil_t[:, 8 * DT :]

    def weights_of(blk0):
        t = jnp.transpose(
            jnp.concatenate([basis[blk0, m], basis[blk0 + 1, m]], axis=0).astype(F32)
        ).reshape(SLOTS, 2, 8, 128)
        lo, hi = t[:, 0], t[:, 1]
        low = low_lanes((SLOTS, 8, 128))
        return (
            jnp.where(low, lo, pltpu.roll(hi.reshape(64, 128), Q, 1).reshape(SLOTS, 8, 128)),
            jnp.where(low, pltpu.roll(lo.reshape(64, 128), Q, 1).reshape(SLOTS, 8, 128), hi),
        )

    def ids_of(blk):
        cols = lanes_at(2 * blk + m // 2, 128)
        v = jnp.where(mask[:, cols] != 0, partner[:, cols] & 255, -1)
        r = pltpu.roll(v, Q, 1)
        odd = m % 2 == 1
        low = low_lanes(v.shape)
        return jnp.where(low, jnp.where(odd, r, v), jnp.where(odd, v, r))

    def spread(k):
        def body(i, carry):
            blk0 = 2 * to_pair(k, i)
            both = weights_of(blk0)
            for half in range(2):
                blk = blk0 + half
                w = both[half]
                for s in range(SLOTS):
                    for j in range(8):
                        wrow[s * 8 + j] = jnp.broadcast_to(w[s, j : j + 1, :], (16, 128)).astype(BF)
                ids = ids_of(blk)

                def part(pt, carry):
                    p_ids = lax.broadcasted_iota(jnp.int32, (32, 128), 0) + 32 * pt
                    acc = [jnp.zeros((2, 16, 128), BF) for _ in range(8)]
                    for s in range(SLOTS):
                        same = (
                            jnp.where(ids[s : s + 1, :] == p_ids, 1.0, 0.0)
                            .astype(BF)
                            .reshape(2, 16, 128)
                        )
                        for j in range(8):
                            acc[j] = acc[j] + same * wrow[s * 8 + j][None]
                    for j in range(8):
                        at[blk, rows_at(pt, 32), 128 * j : 128 * (j + 1)] = acc[j].reshape(32, 128)
                    return carry

                lax.fori_loop(0, 8, part, 0)
            return carry

        lax.fori_loop(0, 4, body, 0)

    def rows_of_x(p):
        return jnp.concatenate([x[j, two(p)].reshape(128, W) for j in range(MP)], axis=1)

    def down(k):
        def body(i, carry):
            p = to_pair(k, i)
            d = lax.dot_general(
                rows_of_x(p), w_down_t[...], (((1,), (1,)), ((), ())), preferred_element_type=F32
            )
            dall[p, rows_at(m, Q), :] = jnp.concatenate([d[:Q], d[Q:]], axis=1).astype(BF)
            return carry

        lax.fori_loop(0, 4, body, 0)

    def hidden(k):
        def body(i, carry):
            p = to_pair(k, i)
            rows = rows_of_x(p)
            total[rows_at(p, 128), :] = rows.astype(F32) + silu(dot(rows, w_full(0)))
            return carry

        lax.fori_loop(0, 4, body, 0)

    def finish(k):
        for i in range(4):
            p = to_pair(k, i)
            dt = jnp.transpose(dall[p].astype(F32)).astype(BF)
            for half in range(2):
                mixed = dot(dt[half * DT : (half + 1) * DT], at[2 * p + half]).astype(BF)
                mix[:, 256 * i + 128 * half : 256 * i + 128 * (half + 1)] = jnp.concatenate(
                    [mixed[:, 128 * j : 128 * (j + 1)] for j in range(8)], axis=0
                )
        o = dot(l_mat[...], mix[...])
        low = low_lanes((DT, 128))
        parts = []
        for i in range(4):
            a, b = o[:, 256 * i : 256 * i + 128], o[:, 256 * i + 128 : 256 * (i + 1)]
            parts.append(
                jnp.where(low, a[:DT] + pltpu.roll(a[DT:], Q, 1), pltpu.roll(b[:DT], Q, 1) + b[DT:])
            )
        up_all = jnp.concatenate([up_f[j] for j in range(MP)], axis=1)
        bil = jnp.transpose(jnp.concatenate(parts, axis=1)).astype(BF)
        for i in range(4):
            p = to_pair(k, i)
            rows = rows_at(p, 128)
            tot = total[rows, :] + dot(bil[128 * i : 128 * (i + 1)], up_all)
            total[rows, :] = tot
            alive = column(pair_row(live, 2 * p, m))
            alive = jnp.concatenate([alive] * 4, axis=1)
            outg[two(p)] = (tot * alive).astype(BF).reshape(2, Q, D)

    def targets(k):
        found = []
        for i in NEAR:
            n = 2 * (4 * k + i)
            p = to_pair(k, i)
            if k == 0 and i == 0:
                found.append((n, 2 * p + 1 - core))
            else:
                found += [(n, 2 * p), (n + 1, 2 * p + 1)]
        return found

    def sources(k):
        found = []
        for i in NEAR:
            p = from_pair(k, i)
            if k == 0 and i == 0:
                found.append(2 * p + 1 - core)
            else:
                found += [2 * p, 2 * p + 1]
        return found

    def graph_copy(q, n, d):
        src, dst = ((outg, incoming), (outg, tbuf), (idq, in_ids))[q]
        return remote(src.at[d], dst.at[g], xs.at[q, n], xr.at[q, g], (d, m))

    def graph_here(q):
        src, dst = ((outg, incoming), (outg, tbuf), (idq, in_ids))[q]
        return pltpu.make_async_copy(src.at[g], dst.at[g], xl.at[q])

    def graph_send(q, k):
        if k == 0:
            graph_here(q).start()
        for n, d in targets(k):
            graph_copy(q, n, d).start()

    def graph_wait(q, k):
        src, dst = ((outg, incoming), (outg, tbuf), (idq, in_ids))[q]
        if k == 0:
            graph_here(q).wait()
        for s in sources(k):
            remote(src.at[s], dst.at[s], xs.at[q, 0], xr.at[q, s], (s, m)).wait_recv()

    def graph_sent(q):
        for k in range(4):
            for n, d in targets(k):
                graph_copy(q, n, d).wait_send()

    spread(ORDER[0])
    for n in range(4):
        w_here(n).wait()
        for j in (2, 1, 3):
            w_copy(n, j).wait_recv()
    for k in range(1, NG):
        w_spread(0, k).start()
    for k in ORDER:
        graph_send(2, k)
    spread(ORDER[1])
    ef_wait(ORDER[0])
    down(ORDER[0])
    down_start(ORDER[0])
    ef_start(ORDER[2])
    w_spread_wait(0)
    hidden(ORDER[0])
    spread(ORDER[2])
    ef_wait(ORDER[1])
    down(ORDER[1])
    down_start(ORDER[1])
    ef_start(ORDER[3])
    down_wait(ORDER[0])
    finish(ORDER[0])
    hidden(ORDER[1])
    graph_send(0, ORDER[0])
    spread(ORDER[3])
    ef_wait(ORDER[2])
    down(ORDER[2])
    down_start(ORDER[2])
    down_wait(ORDER[1])
    finish(ORDER[1])
    hidden(ORDER[2])
    graph_send(0, ORDER[1])
    ef_wait(ORDER[3])
    down(ORDER[3])
    down_start(ORDER[3])
    down_wait(ORDER[2])
    finish(ORDER[2])
    hidden(ORDER[3])
    graph_send(0, ORDER[2])
    down_wait(ORDER[3])
    finish(ORDER[3])
    for k in ORDER:
        graph_wait(2, k)

    def pairs(i, carry):
        a, b = in_ids[2 * i], in_ids[2 * i + 1]
        idr[pl.ds(i, 1), :] = jnp.where(low_lanes(a.shape), a, pltpu.roll(b, Q, 1))
        return carry

    lax.fori_loop(0, NG // 2, pairs, 0)
    graph_send(0, ORDER[3])
    for n in (1, 2):
        for k in range(1, NG):
            w_spread(n, k).start()

    def hot_rows(slot, p, row):
        col = column(row)
        for k in range(n_atoms // 128):
            lane = lax.broadcasted_iota(jnp.int32, (128, 128), 1).astype(F32) + 128.0 * k
            at[slot, 128 * (k // 8) : 128 * (k // 8) + 128, 128 * (k % 8) : 128 * (k % 8) + 128] = (
                jnp.where(col == lane, 1.0, 0.0).astype(BF)
            )

    def hot_targets(k):
        def body(i, carry):
            p = to_pair(k, i)
            hot_rows(4 * k + i, p, idr[pl.ds(p, 1), :])
            return carry

        lax.fori_loop(0, 4, body, 0)

    def hot_sources(k):
        def body(i, carry):
            p = from_pair(k, i)
            hot_rows(16 + 4 * k + i, p, pair_row(source, 2 * p, m) & 2047)
            return carry

        lax.fori_loop(0, 4, body, 0)

    for k in ORDER:
        graph_wait(0, k)

    def part(t, h):
        base = t * quarter + h * h2

        def build(i, carry):
            ids = lax.broadcasted_iota(jnp.int32, (h2, 128), 0) + base
            hot[:, lanes_at(i, 128)] = jnp.where(idr[pl.ds(i, 1), :] == ids, 1.0, 0.0).astype(BF)
            return carry

        lax.fori_loop(0, NG // 2, build, 0)
        tmp[...] = dot(hot[...], incoming[...].reshape(NG * Q, D))
        own_lanes = lanes_at(m, W)
        tmp[:, own_lanes] = tmp[:, own_lanes] + af[
            pl.ds(pl.multiple_of(base, h2), h2), :
        ].astype(F32)
        return tmp[...]

    def p_copy(n):
        t = (up, dn, up, dn, up, dn)[n]
        return remote(pbuf.at[n], rbuf.at[n], ps.at[n], pr.at[n], (g, t))

    pbuf[0] = part(op, 0).astype(BF)
    pbuf[1] = part(op, 1).astype(BF)
    p_copy(0).start()
    part_f[0] = part(up, 0)
    p_copy(1).start()
    part_f[1] = part(dn, 1)
    pbuf[2] = part(up, 1).astype(BF)
    pbuf[3] = part(dn, 0).astype(BF)
    p_copy(2).start()
    p_copy(0).wait_recv()
    pbuf[4] = (part_f[0] + rbuf[0].astype(F32)).astype(BF)
    p_copy(3).start()
    p_copy(1).wait_recv()
    pbuf[5] = (part_f[1] + rbuf[1].astype(F32)).astype(BF)
    p_copy(4).start()
    own[:h2, :] = part(m, 0)
    p_copy(5).start()
    own[h2:, :] = part(m, 1)
    for k in ORDER:
        hot_targets(k)
    w_spread_wait(1)
    graph_sent(0)

    def rows_of(src, h):
        return afull.at[pl.ds(pl.multiple_of(src * quarter + h * h2, h2), h2)]

    def own_copy(h, to):
        t = up if to == 0 else dn
        return remote(rows_of(m, h), rows_of(m, h), us.at[to, h], ur.at[to, h], (g, t))

    def relay(to):
        src, t = (dn, up) if to == 0 else (up, dn)
        return remote(rows_of(src, to), rows_of(src, to), us.at[2, to], ur.at[2, to], (g, t))

    for h in range(2):
        rows = slice(h * h2, (h + 1) * h2)
        a, b = ((3, 4), (2, 5))[h]
        p_copy(a).wait_recv()
        p_copy(b).wait_recv()
        mid = (own[rows, :] + rbuf[a].astype(F32) + rbuf[b].astype(F32)).astype(BF)
        new = (mid.astype(F32) + silu(dot(mid, w_full(1)))).astype(BF)
        afull[pl.ds(pl.multiple_of(m * quarter + h * h2, h2), h2), :] = new
        for to in (h, 1 - h):
            own_copy(h, to).start()
    hot_sources(ORDER[0])
    own_copy(0, 0).wait_recv()
    relay(0).start()
    own_copy(1, 1).wait_recv()
    relay(1).start()
    for k in ORDER[1:]:
        hot_sources(k)
    w_spread_wait(2)
    own_copy(0, 1).wait_recv()
    own_copy(1, 0).wait_recv()
    relay(0).wait_recv()
    relay(1).wait_recv()

    def pick(slot):
        n2 = n_atoms // 2
        hots = at[slot : slot + 4]
        return (
            dot(hots[:, :128].reshape(512, n2), afull[:n2, :])
            + dot(hots[:, 128:].reshape(512, n2), afull[n2:, :])
        ).astype(BF)

    previous = None
    for k in ORDER:
        v = pick(4 * k).reshape(4, 2, Q, D)
        for i in range(4):
            outg[two(to_pair(k, i))] = v[i]
        if previous is not None:
            graph_send(1, previous)
        previous = k
    srcb[...] = pick(16 + 4 * ORDER[0]).reshape(4, 128, D)
    graph_send(1, previous)

    def back(k, i, j):
        p, n = from_pair(k, i), 4 * k + i
        t = (m + j) % MP
        return remote(x.at[t, two(p)], out.at[two(p), m], zs.at[n, j], zr.at[n, j], (g, t))

    def here(k, i):
        p = from_pair(k, i)
        return pltpu.make_async_copy(x.at[m, two(p)], out.at[two(p), m], zl.at[4 * k + i])

    for n, k in enumerate(ORDER):
        if n > 0:
            srcb[...] = pick(16 + 4 * k).reshape(4, 128, D)
        if n == 1:
            aout[...] = afull[:, lanes_at(m, W)]
        graph_wait(1, k)

        def body(i, carry, k=k):
            p = from_pair(k, i)
            pair = (srcb[i].astype(F32) * tbuf[two(p)].reshape(128, D).astype(F32)).astype(BF)
            v = (total[rows_at(p, 128), :] + silu(dot(pair, w_full(2)))).astype(BF)
            for j in range(MP):
                x[j, two(p)] = v[:, W * j : W * (j + 1)].reshape(2, Q, W)
            return carry

        lax.fori_loop(0, 4, body, 0)
        for i in range(4):
            here(k, i).start()
            for j in (2, 1, 3):
                back(k, i, j).start()
    for k in ORDER:
        for i in range(4):
            here(k, i).wait()
            for j in (2, 1, 3):
                back(k, i, j).wait()
                ef_copy(k, i, j).wait_send()
                down_copy(k, i, j).wait_send()
    for n in range(4):
        for j in (2, 1, 3):
            w_copy(n, j).wait_send()
    for n in range(3):
        for k in range(1, NG):
            w_spread(n, k).wait_send()
    graph_sent(1)
    graph_sent(2)
    for n in range(6):
        p_copy(n).wait_send()
    for h in range(2):
        for to in range(2):
            own_copy(h, to).wait_send()
        relay(h).wait_send()


def vmem(shape, dtype):
    return pltpu.VMEM(shape, dtype)


def local(
    edge_feats,
    edge_source,
    edge_target,
    edge_live,
    trip_partner,
    trip_mask,
    trip_basis,
    atom_feats,
    w_msg,
    w_down,
    w_bil,
    w_up,
    w_atom,
    w_edge,
):
    n_edges = edge_feats.shape[0]
    n_atoms = atom_feats.shape[0]
    rows = n_edges // MP
    quarter = n_atoms // MP
    half = quarter // 2
    dma = pltpu.SemaphoreType.DMA
    args = (
        edge_feats.reshape(NG, MP, Q, W),
        edge_target.reshape(2 * NG, 128),
        edge_live.reshape(2 * NG, 128),
        edge_source.reshape(2 * NG, 128),
        trip_partner,
        trip_mask,
        trip_basis.reshape(NG, MP, Q, 128),
        w_msg,
        jnp.transpose(w_down),
        jnp.transpose(w_bil),
        w_up,
        w_atom,
        w_edge,
        atom_feats,
    )
    spec = pl.BlockSpec(memory_space=pltpu.VMEM)
    edge_out, aout = pl.pallas_call(
        block_kernel,
        out_shape=(
            jax.ShapeDtypeStruct((NG, MP, Q, W), BF),
            jax.ShapeDtypeStruct((n_atoms, W), BF),
        ),
        in_specs=[spec] * len(args),
        out_specs=(spec, spec),
        scratch_shapes=[
            vmem((MP, NG, Q, W), BF),
            vmem((NG // 2, CAP, 128), BF),
            vmem((NG, CAP, NB * Q), BF),
            vmem((64, 16, 128), BF),
            vmem((8 * DT, 1024), BF),
            vmem((128, 8 * DT), BF),
            vmem((rows, D), F32),
            vmem((NG, Q, D), BF),
            vmem((NG, Q, D), BF),
            vmem((NG, Q, D), BF),
            vmem((NG, 1, 128), jnp.int32),
            vmem((NG, 1, 128), jnp.int32),
            vmem((NG // 2, 128), jnp.int32),
            vmem((3, MP, D, W), BF),
            vmem((MP, DT, W), BF),
            vmem((half, rows), BF),
            vmem((half, D), F32),
            vmem((2, half, D), F32),
            vmem((quarter, D), F32),
            vmem((6, half, D), BF),
            vmem((6, half, D), BF),
            vmem((n_atoms, D), BF),
            vmem((4, 128, D), BF),
            dma((16, 4)),
            dma((16, 4)),
            dma((16,)),
            dma((16, 4)),
            dma((16, 4)),
            dma((4, 4)),
            dma((4, 4)),
            dma((4,)),
            dma((3, NG)),
            dma((3, NG)),
            dma((3, NG)),
            dma((3, NG)),
            dma((3,)),
            dma((6,)),
            dma((6,)),
            dma((3, 2)),
            dma((3, 2)),
            dma((16, 4)),
            dma((16, 4)),
            dma((16,)),
        ],
        compiler_params=pltpu.CompilerParams(
            collective_id=0, has_side_effects=True, vmem_limit_bytes=62 << 20
        ),
        name="block",
    )(*args)
    return (edge_out.reshape(n_edges, W), aout)


def solution(mesh):
    return jax.shard_map(
        local,
        mesh=mesh,
        in_specs=(
            P("graph", "mp"),
            P("graph"),
            P("graph"),
            P("graph"),
            P(None, "graph"),
            P(None, "graph"),
            P("graph", None),
            P("graph", "mp"),
            P(None, "mp"),
            P(),
            P(),
            P(None, "mp"),
            P(None, "mp"),
            P(None, "mp"),
        ),
        out_specs=(P("graph", "mp"), P("graph", "mp")),
        check_vma=False,
    )
```

time: 532 us -> 169 us (0.32)
  the two profiles are of different devices: /device:TPU:0 before, /device:TPU:13 now
where the time goes in v3:
time: 169 us
  Pallas kernels  164 us (97%)
  local copies, waits for them, and re-layouts  3.9 us (2%)
    pallas_call x1, Pallas kernels, local(): pl.pallas_call(block_kernel, out_shape=(jax.ShapeDtypeStruct((NG, MP, Q,...  164 us
    unnamed x4, local copies, waits for them, and re-layouts  3.9 us

profile of v3, /device:TPU:13, one launch (start us, length us, event | category | flops | bytes accessed | tf_op | source)
XLA Modules:
  0.0 168.9 jit_solution(18349843960935727967)
XLA Ops:
  0.6 164.3 %block.1 = (bf16[32,4,64,128]{3,2,1,0:T(8,128)(2,1)}, bf16[2048,128]{1,0:T(8,128)(2,1)}) custom-call(bf16[32,4,64,128]{3,2,1,0:T(8,128)(2,1)} %bitcast.8, s32[64,128]{1,0:T(8,128)} %bitcast.13, s32[64,128]{1,0:T(8,128)} %bitcast.14, s32[64,128]{1,0:T(8,128)} %bitcast.15, s32[8,8192]{1,0:T(8,128)} %partner.1, s32[8,8192]{1,0:T(8,128)} %mask.1, ...), custom_call_target="tpu_custom_call" | custom-call | tf_op jit(solution)/shard_map/block/pallas_call | solution.py:659
  164.9 0.0 copy-start
  165.0 3.1 %copy.18 = bf16[8192,128]{1,0:T(8,128)(2,1)} copy(bf16[8192,128]{1,0:T(8,128)(2,1)} %bitcast.10) | data formatting | bytes 4194304
  168.1 0.0 copy-done
  168.1 0.8 copy.19
Async XLA Ops:
  164.9 3.1 %copy-start = (bf16[2048,128]{1,0:T(8,128)(2,1)S(1)}, bf16[2048,128]{1,0:T(8,128)(2,1)}, u32[]{:S(2)}) copy-start(bf16[2048,128]{1,0:T(8,128)(2,1)} %get-tuple-element.9) | copy-start | bytes 1572868

commit v4 on v3

--- a/solution.py
+++ b/solution.py
@@ -93,6 +93,7 @@
     dall,
     at,
     wrow,
+    irow,
     mix,
     l_mat,
     total,
@@ -105,13 +106,18 @@
     wf,
     up_f,
     hot,
-    tmp,
+    pacc,
     part_f,
     own,
     pbuf,
     rbuf,
     afull,
     srcb,
+    basis_v,
+    partner_v,
+    mask_v,
+    af_v,
+    il,
     es,
     er,
     el,
@@ -150,6 +156,18 @@
     def two(p):
         return pl.ds(2 * p, 2)
 
+    loads = (
+        (basis.at[:, m], basis_v),
+        (partner, partner_v),
+        (mask, mask_v),
+        (af, af_v),
+    )
+
+    def load(n):
+        return pltpu.make_async_copy(loads[n][0], loads[n][1], il.at[n])
+
+    for n in range(4):
+        load(n).start()
     enter(g, m, True)
 
     def ef_copy(k, i, j):
@@ -235,7 +253,7 @@
 
     def weights_of(blk0):
         t = jnp.transpose(
-            jnp.concatenate([basis[blk0, m], basis[blk0 + 1, m]], axis=0).astype(F32)
+            basis_v[pl.ds(blk0, 2)].reshape(128, 128).astype(F32)
         ).reshape(SLOTS, 2, 8, 128)
         lo, hi = t[:, 0], t[:, 1]
         low = low_lanes((SLOTS, 8, 128))
@@ -246,13 +264,15 @@
 
     def ids_of(blk):
         cols = lanes_at(2 * blk + m // 2, 128)
-        v = jnp.where(mask[:, cols] != 0, partner[:, cols] & 255, -1)
+        v = jnp.where(mask_v[:, cols] != 0, partner_v[:, cols] & 255, -1)
         r = pltpu.roll(v, Q, 1)
         odd = m % 2 == 1
         low = low_lanes(v.shape)
         return jnp.where(low, jnp.where(odd, r, v), jnp.where(odd, v, r))
 
     def spread(k):
+        one, zero = jnp.ones((2, 16, 128), BF), jnp.zeros((2, 16, 128), BF)
+
         def body(i, carry):
             blk0 = 2 * to_pair(k, i)
             both = weights_of(blk0)
@@ -262,19 +282,23 @@
                 for s in range(SLOTS):
                     for j in range(8):
                         wrow[s * 8 + j] = jnp.broadcast_to(w[s, j : j + 1, :], (16, 128)).astype(BF)
-                ids = ids_of(blk)
+                ids = ids_of(blk).astype(F32)
+                for s in range(SLOTS):
+                    irow[s] = jnp.broadcast_to(ids[s : s + 1, :], (16, 128)).astype(BF)
 
                 def part(pt, carry):
-                    p_ids = lax.broadcasted_iota(jnp.int32, (32, 128), 0) + 32 * pt
-                    acc = [jnp.zeros((2, 16, 128), BF) for _ in range(8)]
+                    p_ids = (
+                        (lax.broadcasted_iota(jnp.int32, (32, 128), 0) + 32 * pt)
+                        .astype(F32)
+                        .astype(BF)
+                        .reshape(2, 16, 128)
+                    )
+                    acc = [None] * 8
                     for s in range(SLOTS):
-                        same = (
-                            jnp.where(ids[s : s + 1, :] == p_ids, 1.0, 0.0)
-                            .astype(BF)
-                            .reshape(2, 16, 128)
-                        )
+                        same = jnp.where(irow[s][None] == p_ids, one, zero)
                         for j in range(8):
-                            acc[j] = acc[j] + same * wrow[s * 8 + j][None]
+                            term = same * wrow[s * 8 + j][None]
+                            acc[j] = term if s == 0 else acc[j] + term
                     for j in range(8):
                         at[blk, rows_at(pt, 32), 128 * j : 128 * (j + 1)] = acc[j].reshape(32, 128)
                     return carry
@@ -377,11 +401,12 @@
         for s in sources(k):
             remote(src.at[s], dst.at[s], xs.at[q, 0], xr.at[q, s], (s, m)).wait_recv()
 
-    def graph_sent(q):
-        for k in range(4):
-            for n, d in targets(k):
-                graph_copy(q, n, d).wait_send()
-
+    def graph_sent(q, k):
+        for n, d in targets(k):
+            graph_copy(q, n, d).wait_send()
+
+    for n in range(3):
+        load(n).wait()
     spread(ORDER[0])
     for n in range(4):
         w_here(n).wait()
@@ -391,14 +416,13 @@
         w_spread(0, k).start()
     for k in ORDER:
         graph_send(2, k)
-    spread(ORDER[1])
     ef_wait(ORDER[0])
     down(ORDER[0])
     down_start(ORDER[0])
     ef_start(ORDER[2])
+    spread(ORDER[1])
     w_spread_wait(0)
     hidden(ORDER[0])
-    spread(ORDER[2])
     ef_wait(ORDER[1])
     down(ORDER[1])
     down_start(ORDER[1])
@@ -407,7 +431,7 @@
     finish(ORDER[0])
     hidden(ORDER[1])
     graph_send(0, ORDER[0])
-    spread(ORDER[3])
+    spread(ORDER[2])
     ef_wait(ORDER[2])
     down(ORDER[2])
     down_start(ORDER[2])
@@ -415,17 +439,18 @@
     finish(ORDER[1])
     hidden(ORDER[2])
     graph_send(0, ORDER[1])
+    spread(ORDER[3])
     ef_wait(ORDER[3])
     down(ORDER[3])
     down_start(ORDER[3])
+    for k in ORDER:
+        graph_wait(2, k)
     down_wait(ORDER[2])
     finish(ORDER[2])
     hidden(ORDER[3])
     graph_send(0, ORDER[2])
     down_wait(ORDER[3])
     finish(ORDER[3])
-    for k in ORDER:
-        graph_wait(2, k)
 
     def pairs(i, carry):
         a, b = in_ids[2 * i], in_ids[2 * i + 1]
@@ -434,9 +459,6 @@
 
     lax.fori_loop(0, NG // 2, pairs, 0)
     graph_send(0, ORDER[3])
-    for n in (1, 2):
-        for k in range(1, NG):
-            w_spread(n, k).start()
 
     def hot_rows(slot, p, row):
         col = column(row)
@@ -462,24 +484,39 @@
 
         lax.fori_loop(0, 4, body, 0)
 
-    for k in ORDER:
+    def chunk_dot(th, k):
+        base = th * h2
+        for i in range(4):
+            ids = lax.broadcasted_iota(jnp.int32, (h2, 128), 0) + base
+            hot[:, 128 * i : 128 * (i + 1)] = jnp.where(
+                idr[pl.ds(from_pair(k, i), 1), :] == ids, 1.0, 0.0
+            ).astype(BF)
+        rows = jnp.concatenate(
+            [incoming[two(from_pair(k, i))].reshape(128, D) for i in range(4)], axis=0
+        )
+        return dot(hot[...], rows)
+
+    load(3).wait()
+
+    def seed(th, carry):
+        pacc[th] = jnp.zeros((h2, D), F32)
+        pacc[th, :, lanes_at(m, W)] = af_v[rows_at(th, h2), :].astype(F32)
+        return carry
+
+    lax.fori_loop(0, 2 * MP, seed, 0)
+    for k in ORDER[:3]:
         graph_wait(0, k)
 
+        def gather(th, carry, k=k):
+            pacc[th] = pacc[th] + chunk_dot(th, k)
+            return carry
+
+        lax.fori_loop(0, 2 * MP, gather, 0)
+    graph_wait(0, ORDER[3])
+
     def part(t, h):
-        base = t * quarter + h * h2
-
-        def build(i, carry):
-            ids = lax.broadcasted_iota(jnp.int32, (h2, 128), 0) + base
-            hot[:, lanes_at(i, 128)] = jnp.where(idr[pl.ds(i, 1), :] == ids, 1.0, 0.0).astype(BF)
-            return carry
-
-        lax.fori_loop(0, NG // 2, build, 0)
-        tmp[...] = dot(hot[...], incoming[...].reshape(NG * Q, D))
-        own_lanes = lanes_at(m, W)
-        tmp[:, own_lanes] = tmp[:, own_lanes] + af[
-            pl.ds(pl.multiple_of(base, h2), h2), :
-        ].astype(F32)
-        return tmp[...]
+        th = 2 * t + h
+        return pacc[th] + chunk_dot(th, ORDER[3])
 
     def p_copy(n):
         t = (up, dn, up, dn, up, dn)[n]
@@ -494,19 +531,23 @@
     pbuf[2] = part(up, 1).astype(BF)
     pbuf[3] = part(dn, 0).astype(BF)
     p_copy(2).start()
+    own[:h2, :] = part(m, 0)
+    p_copy(3).start()
+    own[h2:, :] = part(m, 1)
+    for n in (1, 2):
+        for k in range(1, NG):
+            w_spread(n, k).start()
     p_copy(0).wait_recv()
     pbuf[4] = (part_f[0] + rbuf[0].astype(F32)).astype(BF)
-    p_copy(3).start()
     p_copy(1).wait_recv()
     pbuf[5] = (part_f[1] + rbuf[1].astype(F32)).astype(BF)
     p_copy(4).start()
-    own[:h2, :] = part(m, 0)
     p_copy(5).start()
-    own[h2:, :] = part(m, 1)
     for k in ORDER:
         hot_targets(k)
     w_spread_wait(1)
-    graph_sent(0)
+    for k in ORDER:
+        graph_sent(0, k)
 
     def rows_of(src, h):
         return afull.at[pl.ds(pl.multiple_of(src * quarter + h * h2, h2), h2)]
@@ -539,8 +580,6 @@
     w_spread_wait(2)
     own_copy(0, 1).wait_recv()
     own_copy(1, 0).wait_recv()
-    relay(0).wait_recv()
-    relay(1).wait_recv()
 
     def pick(slot):
         n2 = n_atoms // 2
@@ -550,16 +589,27 @@
             + dot(hots[:, 128:].reshape(512, n2), afull[n2:, :])
         ).astype(BF)
 
-    previous = None
+    def pick_from(slot, t):
+        hots = at[slot : slot + 4, pl.ds(pl.multiple_of((t // 2) * 128, 128), 128), lanes_at(t % 2, 512)]
+        return dot(hots.reshape(512, quarter), afull[rows_at(t, quarter), :])
+
     for k in ORDER:
-        v = pick(4 * k).reshape(4, 2, Q, D)
+        v = (pick_from(4 * k, m) + pick_from(4 * k, up) + pick_from(4 * k, dn)).astype(BF)
+        v = v.reshape(4, 2, Q, D)
         for i in range(4):
             outg[two(to_pair(k, i))] = v[i]
-        if previous is not None:
-            graph_send(1, previous)
-        previous = k
+    relay(0).wait_recv()
+    relay(1).wait_recv()
+    for n, k in enumerate(ORDER):
+        v = pick_from(4 * k, op).astype(BF).reshape(4, 2, Q, D)
+        for i in range(4):
+            p = two(to_pair(k, i))
+            outg[p] = outg[p] + v[i]
+        if 0 < n < 3:
+            graph_send(1, ORDER[n - 1])
     srcb[...] = pick(16 + 4 * ORDER[0]).reshape(4, 128, D)
-    graph_send(1, previous)
+    graph_sent(1, ORDER[0])
+    graph_send(1, ORDER[2])
 
     def back(k, i, j):
         p, n = from_pair(k, i), 4 * k + i
@@ -575,21 +625,34 @@
             srcb[...] = pick(16 + 4 * k).reshape(4, 128, D)
         if n == 1:
             aout[...] = afull[:, lanes_at(m, W)]
-        graph_wait(1, k)
-
         def body(i, carry, k=k):
+            p = from_pair(k, i)
+            for s in (2 * p, 2 * p + 1):
+                remote(outg.at[s], tbuf.at[s], xs.at[1, 0], xr.at[1, s], (s, m)).wait_recv()
+            return edge_rows(k, i, carry)
+
+        def edge_rows(k, i, carry):
             p = from_pair(k, i)
             pair = (srcb[i].astype(F32) * tbuf[two(p)].reshape(128, D).astype(F32)).astype(BF)
             v = (total[rows_at(p, 128), :] + silu(dot(pair, w_full(2)))).astype(BF)
             for j in range(MP):
                 x[j, two(p)] = v[:, W * j : W * (j + 1)].reshape(2, Q, W)
-            return carry
-
-        lax.fori_loop(0, 4, body, 0)
-        for i in range(4):
             here(k, i).start()
             for j in (2, 1, 3):
                 back(k, i, j).start()
+            return carry
+
+        if k == 0:
+            graph_here(1).wait()
+            s = g + 1 - 2 * core
+            remote(outg.at[s], tbuf.at[s], xs.at[1, 0], xr.at[1, s], (s, m)).wait_recv()
+            edge_rows(0, 0, 0)
+            lax.fori_loop(1, 4, body, 0)
+        else:
+            lax.fori_loop(0, 4, body, 0)
+        if n == 0:
+            graph_sent(1, ORDER[1])
+            graph_send(1, ORDER[3])
     for k in ORDER:
         for i in range(4):
             here(k, i).wait()
@@ -603,8 +666,10 @@
     for n in range(3):
         for k in range(1, NG):
             w_spread(n, k).wait_send()
-    graph_sent(1)
-    graph_sent(2)
+    for k in ORDER:
+        graph_sent(2, k)
+    for k in ORDER[2:]:
+        graph_sent(1, k)
     for n in range(6):
         p_copy(n).wait_send()
     for h in range(2):
@@ -656,19 +721,21 @@
         atom_feats,
     )
     spec = pl.BlockSpec(memory_space=pltpu.VMEM)
+    hbm = pl.BlockSpec(memory_space=pl.ANY)
     edge_out, aout = pl.pallas_call(
         block_kernel,
         out_shape=(
             jax.ShapeDtypeStruct((NG, MP, Q, W), BF),
             jax.ShapeDtypeStruct((n_atoms, W), BF),
         ),
-        in_specs=[spec] * len(args),
-        out_specs=(spec, spec),
+        in_specs=[hbm, spec, spec, spec, hbm, hbm, hbm, hbm, spec, spec, hbm, hbm, hbm, hbm],
+        out_specs=(hbm, spec),
         scratch_shapes=[
             vmem((MP, NG, Q, W), BF),
             vmem((NG // 2, CAP, 128), BF),
             vmem((NG, CAP, NB * Q), BF),
             vmem((64, 16, 128), BF),
+            vmem((SLOTS, 16, 128), BF),
             vmem((8 * DT, 1024), BF),
             vmem((128, 8 * DT), BF),
             vmem((rows, D), F32),
@@ -680,14 +747,19 @@
             vmem((NG // 2, 128), jnp.int32),
             vmem((3, MP, D, W), BF),
             vmem((MP, DT, W), BF),
-            vmem((half, rows), BF),
-            vmem((half, D), F32),
+            vmem((half, 512), BF),
+            vmem((2 * MP, half, D), F32),
             vmem((2, half, D), F32),
             vmem((quarter, D), F32),
             vmem((6, half, D), BF),
             vmem((6, half, D), BF),
             vmem((n_atoms, D), BF),
             vmem((4, 128, D), BF),
+            vmem((NG, Q, 128), BF),
+            vmem((SLOTS, n_edges), jnp.int32),
+            vmem((SLOTS, n_edges), jnp.int32),
+            vmem((n_atoms, W), BF),
+            dma((4,)),
             dma((16, 4)),
             dma((16, 4)),
             dma((16,)),

time: 169 us -> 160 us (0.947)
  the two profiles are of different devices: /device:TPU:13 before, /device:TPU:0 now
where the time goes in v4:
time: 160 us; the launch traced here: 158 us
  Pallas kernels  153 us (96%)
  local copies, waits for them, and re-layouts  3.9 us (2%)
    pallas_call x1, Pallas kernels, local(): pl.pallas_call(block_kernel, out_shape=(jax.ShapeDtypeStruct((NG, MP, Q,...  153 us
    unnamed x4, local copies, waits for them, and re-layouts  3.9 us

profile of v4, /device:TPU:0, one launch (start us, length us, event | category | flops | bytes accessed | tf_op | source)
XLA Modules:
  0.0 157.8 jit_solution(7414144419274783556)
XLA Ops:
  0.6 153.3 %block.1 = (bf16[32,4,64,128]{3,2,1,0:T(8,128)(2,1)}, bf16[2048,128]{1,0:T(8,128)(2,1)}) custom-call(bf16[32,4,64,128]{3,2,1,0:T(8,128)(2,1)} %bitcast.8, s32[64,128]{1,0:T(8,128)} %bitcast.13, s32[64,128]{1,0:T(8,128)} %bitcast.14, s32[64,128]{1,0:T(8,128)} %bitcast.15, s32[8,8192]{1,0:T(8,128)} %partner.1, s32[8,8192]{1,0:T(8,128)} %mask.1, ...), custom_call_target="tpu_custom_call" | custom-call | tf_op jit(solution)/shard_map/block/pallas_call | solution.py:725
  153.9 0.0 copy-start
  153.9 3.1 %copy.18 = bf16[8192,128]{1,0:T(8,128)(2,1)} copy(bf16[8192,128]{1,0:T(8,128)(2,1)} %bitcast.10) | data formatting | bytes 4194304
  157.0 0.0 copy-done
  157.0 0.8 copy.19
Async XLA Ops:
  153.9 3.1 %copy-start = (bf16[2048,128]{1,0:T(8,128)(2,1)S(1)}, bf16[2048,128]{1,0:T(8,128)(2,1)}, u32[]{:S(2)}) copy-start(bf16[2048,128]{1,0:T(8,128)(2,1)} %get-tuple-element.9) | copy-start | bytes 1572868

commit v5 on v4

--- a/solution.py
+++ b/solution.py
@@ -429,16 +429,16 @@
     ef_start(ORDER[3])
     down_wait(ORDER[0])
     finish(ORDER[0])
+    graph_send(0, ORDER[0])
     hidden(ORDER[1])
-    graph_send(0, ORDER[0])
     spread(ORDER[2])
     ef_wait(ORDER[2])
     down(ORDER[2])
     down_start(ORDER[2])
     down_wait(ORDER[1])
     finish(ORDER[1])
+    graph_send(0, ORDER[1])
     hidden(ORDER[2])
-    graph_send(0, ORDER[1])
     spread(ORDER[3])
     ef_wait(ORDER[3])
     down(ORDER[3])
@@ -447,8 +447,8 @@
         graph_wait(2, k)
     down_wait(ORDER[2])
     finish(ORDER[2])
+    graph_send(0, ORDER[2])
     hidden(ORDER[3])
-    graph_send(0, ORDER[2])
     down_wait(ORDER[3])
     finish(ORDER[3])
 

time: 160 us -> 160 us (level); the launches traced: 158 us -> 160 us
  Pallas kernels: 153 us -> 155 us
    pallas_call x1, Pallas kernels: 153 us -> 155 us  [local(): pl.pallas_call(block_kernel, out_shape=(jax.ShapeDtypeStruct((NG, MP, Q,...]
where the time goes in v5:
time: 160 us
  Pallas kernels  155 us (97%)
  local copies, waits for them, and re-layouts  3.9 us (2%)
    pallas_call x1, Pallas kernels, local(): pl.pallas_call(block_kernel, out_shape=(jax.ShapeDtypeStruct((NG, MP, Q,...  155 us
    unnamed x4, local copies, waits for them, and re-layouts  3.9 us

profile of v5, /device:TPU:0, one launch (start us, length us, event | category | flops | bytes accessed | tf_op | source)
XLA Modules:
  0.0 159.8 jit_solution(6895644684272909600)
XLA Ops:
  0.6 155.3 %block.1 = (bf16[32,4,64,128]{3,2,1,0:T(8,128)(2,1)}, bf16[2048,128]{1,0:T(8,128)(2,1)}) custom-call(bf16[32,4,64,128]{3,2,1,0:T(8,128)(2,1)} %bitcast.8, s32[64,128]{1,0:T(8,128)} %bitcast.13, s32[64,128]{1,0:T(8,128)} %bitcast.14, s32[64,128]{1,0:T(8,128)} %bitcast.15, s32[8,8192]{1,0:T(8,128)} %partner.1, s32[8,8192]{1,0:T(8,128)} %mask.1, ...), custom_call_target="tpu_custom_call" | custom-call | tf_op jit(solution)/shard_map/block/pallas_call | solution.py:725
  155.9 0.0 copy-start
  155.9 3.1 %copy.18 = bf16[8192,128]{1,0:T(8,128)(2,1)} copy(bf16[8192,128]{1,0:T(8,128)(2,1)} %bitcast.10) | data formatting | bytes 4194304
  159.0 0.0 copy-done
  159.0 0.8 copy.19
Async XLA Ops:
  155.9 3.1 %copy-start = (bf16[2048,128]{1,0:T(8,128)(2,1)S(1)}, bf16[2048,128]{1,0:T(8,128)(2,1)}, u32[]{:S(2)}) copy-start(bf16[2048,128]{1,0:T(8,128)(2,1)} %get-tuple-element.9) | copy-start | bytes 1572868
